TPU v7x, 32 devices: a whole 2x2x4 slice. The times are simulated.
32 devices in a mesh: dp: 4 (over y, x), mp: 8 (over z, core).
Axes of the slice: x: 2, y: 2, z: 4, core: 2. Of those that a mesh axis runs over, the one named last changes fastest.
Arguments:
- features: bfloat16 [1536, 8192], P('dp', 'mp'), may hold values from -6 to 6
- cotangent: bfloat16 [1536, 8192], P('dp', 'mp'), may hold values from -6 to 6
- weights: bfloat16 [2, 8192, 8192], P(None, 'mp'), may hold values from -0.0625 to 0.0625
- biases: float32 [2, 8192], P(None, 'mp'), may hold values from -3 to 3
- weight_accum: float32 [2, 8192], P(None, ('mp', 'dp')), may hold values from 100 to 16000
- owner_slot: int32 [128], replicated, may hold values from 0 to 127, each once
- bag_ids: int32 [128, 1536, 4], P(('dp', 'mp')), may hold values from 0 to 8191
- bag_length: int32 [128, 1536], P(('dp', 'mp')), may hold values from 1 to 4, as said below
- tables: float32 [128, 8192, 64], P(('dp', 'mp')), may hold values from -3 to 3
- table_accum: float32 [128, 8192], P(('dp', 'mp')), may hold values from 1 to 256
Outputs:
- weight_step: float32 [2, 8192, 8192], P(None, ('mp', 'dp'))
- new_weight_accum: float32 [2, 8192], P(None, ('mp', 'dp'))
- new_tables: float32 [128, 8192, 64], P(('dp', 'mp'))
- new_table_accum: float32 [128, 8192], P(('dp', 'mp'))
Inputs may be any that keep to these rules, and one draw needn't show every extreme that they name: `owner_slot`: A permutation; the owner slot s lies on device s // 4 in the order of dp+mp, as its entry s % 4. Only the first bag_length ids of a bag are looked up.
All inputs are finite; a program needn't handle non-finite values.
Results may differ from a plain program's by a relative error of at most 0.025.
Values may be sent and summed in bfloat16 or wider, within the bound.
No kernel may reach another device: no remote copies, remote signals or barrier semaphores. Data moves between devices by JAX's collectives and lax.ppermute only.
A program may use at most 192 MiB of HBM per device.

v0:
```python
import functools
import jax, jax.numpy as jnp
from jax import lax
from jax.experimental import pallas as pl
from jax.experimental.pallas import tpu as pltpu
from jax.sharding import PartitionSpec as P


learn_rate = 0.5
cores = 2


def embed_kernel(n_tab, bag, batch, vocab, embed, chunk, unroll, rate, ids_ref, g_ref, tab_ref, acc_in_ref, tab_out, acc_out, rows, *accs):
    step = pl.program_id(0)
    pairs = g_ref.shape[1]

    @pl.when(step == 0)
    def _():
        src, _, per, lanes = g_ref.shape
        piece = min(256, vocab)

        def clear(i, carry):
            start = pl.multiple_of(i * piece, piece)
            for a in accs:
                a[pl.ds(start, piece), :] = jnp.zeros((piece, a.shape[1]), jnp.float32)
            return carry

        lax.fori_loop(0, vocab // piece, clear, 0)
        for p in range(pairs):
            rows[p] = g_ref[:, p].astype(jnp.float32).reshape(src * per, lanes)

        def one(i, carry):
            for u in range(unroll):
                b = i * unroll + u
                vals = [rows[p, pl.ds(b, 1), :] for p in range(pairs)]
                for j in range(bag):
                    for t in range(n_tab):
                        v = ids_ref[(t * bag + j) * batch + b]
                        accs[t + n_tab * (j % 2)][pl.ds(v, 1), :] += vals[t // 2]
            return carry

        lax.fori_loop(0, batch // unroll, one, 0)

    base = pl.multiple_of(step * chunk, chunk)
    for p in range(pairs):
        first = accs[2 * p][pl.ds(base, chunk), :] + accs[n_tab + 2 * p][pl.ds(base, chunk), :]
        if 2 * p + 1 < n_tab:
            second = accs[2 * p + 1][pl.ds(base, chunk), :] + accs[n_tab + 2 * p + 1][pl.ds(base, chunk), :]
            lane = lax.broadcasted_iota(jnp.int32, first.shape, 1)
            first = jnp.where(lane < embed, first, second)
        turned = first.T
        for o in range(min(2, n_tab - 2 * p)):
            t = 2 * p + o
            grad = turned[o * embed:(o + 1) * embed, :]
            renewed = acc_in_ref[t:t + 1, :] + jnp.sum(grad * grad, axis=0, keepdims=True) * (1.0 / embed)
            acc_out[t:t + 1, :] = renewed
            tab_out[t] = tab_ref[t] - grad * (rate / jnp.sqrt(renewed))


def embed_update(ids, grads, tables_t, accum, bag, batch, rate, chunk=2048, unroll=8):
    n_tab, embed, vocab = tables_t.shape
    chunk = min(chunk, vocab)
    kern = functools.partial(embed_kernel, n_tab, bag, batch, vocab, embed, chunk, unroll, rate)
    return pl.pallas_call(
        kern,
        out_shape=(jax.ShapeDtypeStruct(tables_t.shape, jnp.float32), jax.ShapeDtypeStruct(accum.shape, jnp.float32)),
        grid_spec=pltpu.PrefetchScalarGridSpec(
            num_scalar_prefetch=1,
            grid=(vocab // chunk,),
            in_specs=[
                pl.BlockSpec(grads.shape, lambda i, s: (0,) * 4, pipeline_mode=pl.Buffered(1)),
                pl.BlockSpec((n_tab, embed, chunk), lambda i, s: (0, 0, i)),
                pl.BlockSpec((n_tab, chunk), lambda i, s: (0, i)),
            ],
            out_specs=[
                pl.BlockSpec((n_tab, embed, chunk), lambda i, s: (0, 0, i)),
                pl.BlockSpec((n_tab, chunk), lambda i, s: (0, i)),
            ],
            scratch_shapes=[pltpu.VMEM((grads.shape[1], batch, grads.shape[3]), jnp.float32)]
            + [pltpu.VMEM((vocab + 8, grads.shape[3]), jnp.float32) for _ in range(2 * n_tab)],
        ),
        compiler_params=pltpu.CompilerParams(dimension_semantics=("arbitrary",), vmem_limit_bytes=56 * 1024 * 1024),
        cost_estimate=pl.CostEstimate(flops=100000000, bytes_accessed=150000000, transcendentals=0),
        name="embed_update",
    )(ids, grads, tables_t, accum)


def tile_of(size, limit):
    return max(t for t in range(128, limit + 1, 128) if size % t == 0)


def turn_kernel(parts, index_ref, value_ref, turned_ref, own_ref, other_ref):
    share = own_ref.shape[1]
    width = value_ref.shape[1]
    for first in range(0, width, 128):
        turned_ref[first : first + 128, :] = value_ref[:, first : first + 128].T
    for which, out in enumerate((own_ref, other_ref)):
        for k in range(parts):
            start = pl.multiple_of(index_ref[which * parts + k] * share, share)
            out[k] = turned_ref[pl.ds(start, share), :]


def turn(sent_index, value, parts, share):
    rows, width = value.shape
    return pl.pallas_call(
        functools.partial(turn_kernel, parts),
        out_shape=[
            jax.ShapeDtypeStruct((width, rows), value.dtype),
            jax.ShapeDtypeStruct((parts, share, rows), value.dtype),
            jax.ShapeDtypeStruct((parts, share, rows), value.dtype),
        ],
        grid_spec=pltpu.PrefetchScalarGridSpec(
            num_scalar_prefetch=1,
            grid=(1,),
            in_specs=[pl.BlockSpec((rows, width), lambda i, s: (0, 0))],
            out_specs=[
                pl.BlockSpec((width, rows), lambda i, s: (0, 0)),
                pl.BlockSpec((parts, share, rows), lambda i, s: (0, 0, 0)),
                pl.BlockSpec((parts, share, rows), lambda i, s: (0, 0, 0)),
            ],
        ),
        compiler_params=pltpu.CompilerParams(vmem_limit_bytes=16 * 1024 * 1024),
        cost_estimate=pl.CostEstimate(
            flops=rows * width, bytes_accessed=8 * rows * width, transcendentals=0
        ),
        name="turn",
    )(sent_index, value)


def grad_kernel(parts, index_ref, *refs):
    mine, near = refs[:parts], refs[parts]
    own, nxt = refs[parts + 1][...], refs[parts + 2][...]
    outs = refs[parts + 3 :]
    for k in range(parts):
        total = jnp.dot(mine[k][...], own, preferred_element_type=jnp.float32)
        total = total + jnp.dot(near[k], nxt, preferred_element_type=jnp.float32)
        outs[k][...] = total.astype(outs[k].dtype)


def half_grad(index, turned, near, wide, next_half):
    parts, share, rows = near.shape
    half = next_half.shape[1]
    tile = tile_of(half, 1024)
    per_half = half // tile

    def chosen(k):
        return pl.BlockSpec((share, rows), lambda i, s: (s[1 + k], 0))

    return pl.pallas_call(
        functools.partial(grad_kernel, parts),
        out_shape=[jax.ShapeDtypeStruct((share, half), jnp.bfloat16) for _ in range(parts)],
        grid_spec=pltpu.PrefetchScalarGridSpec(
            num_scalar_prefetch=1,
            grid=(per_half,),
            in_specs=[chosen(k) for k in range(parts)]
            + [
                pl.BlockSpec(near.shape, lambda i, s: (0, 0, 0)),
                pl.BlockSpec((rows, tile), lambda i, s: (0, s[0] * per_half + i)),
                pl.BlockSpec((rows, tile), lambda i, s: (0, i)),
            ],
            out_specs=[pl.BlockSpec((share, tile), lambda i, s: (0, i)) for _ in range(parts)],
        ),
        compiler_params=pltpu.CompilerParams(vmem_limit_bytes=32 * 1024 * 1024),
        cost_estimate=pl.CostEstimate(
            flops=4 * parts * share * rows * half,
            bytes_accessed=4 * rows * half + 2 * parts * share * half,
            transcendentals=0,
        ),
        name="half_grad",
    )(index, *([turned] * parts), near, wide, next_half)


def copy_kernel(index_ref, value_ref, out_ref):
    out_ref[...] = value_ref[...]


def column_half(side, value):
    rows, width = value.shape
    half = width // 2
    tile = rows // 4
    return pl.pallas_call(
        copy_kernel,
        out_shape=jax.ShapeDtypeStruct((rows, half), value.dtype),
        grid_spec=pltpu.PrefetchScalarGridSpec(
            num_scalar_prefetch=1,
            grid=(4,),
            in_specs=[pl.BlockSpec((tile, half), lambda i, s: (i, s[0]))],
            out_specs=pl.BlockSpec((tile, half), lambda i, s: (i, 0)),
        ),
        cost_estimate=pl.CostEstimate(
            flops=0, bytes_accessed=4 * rows * half, transcendentals=0
        ),
        name="column_half",
    )(side, value)


def columns_kernel(index_ref, value_ref, weight_ref, out_ref):
    out_ref[0] = jnp.dot(
        value_ref[...], weight_ref[0], preferred_element_type=jnp.float32
    ).astype(out_ref.dtype)


def column_blocks(index, value, weights, layer_idx, width):
    rows, depth = value.shape
    count = index.shape[0]
    tile = tile_of(width, 1024)
    steps = width // tile
    return pl.pallas_call(
        columns_kernel,
        out_shape=jax.ShapeDtypeStruct((count, rows, width), value.dtype),
        grid_spec=pltpu.PrefetchScalarGridSpec(
            num_scalar_prefetch=1,
            grid=(count, steps),
            in_specs=[
                pl.BlockSpec((rows, depth), lambda b, t, s: (0, 0)),
                pl.BlockSpec((1, depth, tile), lambda b, t, s: (layer_idx, 0, s[b] * steps + t)),
            ],
            out_specs=pl.BlockSpec((1, rows, tile), lambda b, t, s: (b, 0, t)),
        ),
        compiler_params=pltpu.CompilerParams(vmem_limit_bytes=24 * 1024 * 1024),
        cost_estimate=pl.CostEstimate(
            flops=2 * rows * depth * width * count,
            bytes_accessed=2 * width * count * (depth + rows),
            transcendentals=0,
        ),
        name="column_blocks",
    )(index, value, weights)


def rows_kernel(count, index_ref, *refs):
    weight_ref, out_ref = refs[count], refs[count + 1]
    value = jnp.concatenate([ref[...] for ref in refs[:count]], axis=0)
    product = jnp.dot(value, weight_ref[0], preferred_element_type=jnp.float32)
    out_ref[...] = product.astype(out_ref.dtype).reshape(out_ref.shape)


def row_blocks_product(index, value, weights, layer_idx):
    count = index.shape[0]
    rows, depth = value.shape
    size = rows // count
    width = weights.shape[2]
    tile = tile_of(width, 1024)

    def chosen(k):
        return pl.BlockSpec((size, depth), lambda i, s: (s[k], 0))

    return pl.pallas_call(
        functools.partial(rows_kernel, count),
        out_shape=jax.ShapeDtypeStruct((count, size, width), value.dtype),
        grid_spec=pltpu.PrefetchScalarGridSpec(
            num_scalar_prefetch=1,
            grid=(width // tile,),
            in_specs=[chosen(k) for k in range(count)]
            + [pl.BlockSpec((1, depth, tile), lambda i, s: (layer_idx, 0, i))],
            out_specs=pl.BlockSpec((count, size, tile), lambda i, s: (0, 0, i)),
        ),
        compiler_params=pltpu.CompilerParams(vmem_limit_bytes=24 * 1024 * 1024),
        cost_estimate=pl.CostEstimate(
            flops=2 * rows * depth * width,
            bytes_accessed=2 * width * (depth + rows),
            transcendentals=0,
        ),
        name="row_blocks_product",
    )(index, *([value] * count), weights)


def forward_kernel(wide_ref, weight_ref, bias_ref, out_ref):
    @pl.when(pl.program_id(0) == 0)
    def _():
        out_ref[...] = jnp.broadcast_to(bias_ref[...], out_ref.shape)

    out_ref[...] += lax.dot_general(
        wide_ref[...],
        weight_ref[0],
        (((1,), (1,)), ((), ())),
        preferred_element_type=jnp.float32,
    )


def forward_product(wide, weights, bias, layer_idx):
    rows, full = wide.shape
    width = weights.shape[1]
    tile = tile_of(full, 1024)
    return pl.pallas_call(
        forward_kernel,
        out_shape=jax.ShapeDtypeStruct((rows, width), jnp.float32),
        grid=(full // tile,),
        in_specs=[
            pl.BlockSpec((rows, tile), lambda i: (0, i)),
            pl.BlockSpec((1, width, tile), lambda i: (layer_idx, 0, i)),
            pl.BlockSpec((1, width), lambda i: (0, 0)),
        ],
        out_specs=pl.BlockSpec((rows, width), lambda i: (0, 0)),
        compiler_params=pltpu.CompilerParams(vmem_limit_bytes=24 * 1024 * 1024),
        cost_estimate=pl.CostEstimate(
            flops=2 * rows * full * width,
            bytes_accessed=2 * full * (rows + width),
            transcendentals=0,
        ),
        name="forward_product",
    )(wide, weights, bias[None])


def blank(shape):
    return pl.pallas_call(
        lambda out_ref: None,
        out_shape=jax.ShapeDtypeStruct(shape, jnp.bfloat16),
        out_specs=pl.BlockSpec(memory_space=pl.ANY),
    )()


def after(value, *needed):
    return lax.optimization_barrier((value, *needed))[0]


def step_kernel(parts, side_ref, accum_ref, *refs):
    pieces, out_ref, new_ref = refs[: 2 * parts], refs[-2], refs[-1]
    width = out_ref.shape[2]
    half = width // 2
    sums = []
    for h in range(2):
        total = pieces[h * parts][...].astype(jnp.float32)
        for k in range(1, parts):
            total = total + pieces[h * parts + k][...].astype(jnp.float32)
        sums.append(total)
    square = jnp.sum(sums[0] * sums[0], axis=1, keepdims=True) + jnp.sum(
        sums[1] * sums[1], axis=1, keepdims=True
    )
    renewed = accum_ref[...] + square * (1.0 / width)
    new_ref[...] = renewed
    scale = 1.0 / jnp.sqrt(renewed)
    side = side_ref[0]
    near = pl.multiple_of(side * half, 128)
    far = pl.multiple_of((1 - side) * half, 128)
    out_ref[0, :, pl.ds(near, half)] = sums[0] * scale
    out_ref[0, :, pl.ds(far, half)] = sums[1] * scale


def weight_update(side, accum, near_parts, far_parts, layer_idx, depth, whole):
    parts = len(near_parts)
    share, half = near_parts[0].shape
    tile = 32
    piece = pl.BlockSpec((tile, half), lambda i, s: (i, 0))
    single = pl.BlockSpec((tile, 1), lambda i, s: (i, 0))
    carried = [] if whole is None else [whole]
    return pl.pallas_call(
        functools.partial(step_kernel, parts),
        out_shape=[
            jax.ShapeDtypeStruct((depth, share, 2 * half), jnp.float32),
            jax.ShapeDtypeStruct((share, 1), jnp.float32),
        ],
        grid_spec=pltpu.PrefetchScalarGridSpec(
            num_scalar_prefetch=1,
            grid=(share // tile,),
            in_specs=[single] + [piece] * (2 * parts) + [pl.BlockSpec(memory_space=pl.ANY)] * len(carried),
            out_specs=[
                pl.BlockSpec((1, tile, 2 * half), lambda i, s: (layer_idx, i, 0)),
                single,
            ],
        ),
        input_output_aliases={2 + 2 * parts: 0} if carried else {},
        compiler_params=pltpu.CompilerParams(vmem_limit_bytes=32 * 1024 * 1024),
        cost_estimate=pl.CostEstimate(
            flops=8 * share * half,
            bytes_accessed=share * half * (8 + 4 * parts),
            transcendentals=0,
        ),
        name="weight_update",
    )(side, accum, *near_parts, *far_parts, *carried)


def slot_kernel(embed, per_device, table_ref, summed_ref, late_ref, out_ref, joined):
    width = late_ref.shape[2]
    for m in range(late_ref.shape[0]):
        cols = slice(m * width, (m + 1) * width)
        joined[:, cols] = summed_ref[:, cols] + late_ref[m].astype(jnp.float32)
    devices, pairs, rows, lanes = out_ref.shape
    lane = lax.broadcasted_iota(jnp.int32, (rows, lanes), 1)

    def look(slot):
        first = table_ref[slot] * embed
        start = pl.multiple_of(first // lanes * lanes, 128)
        value = joined[:, pl.ds(start, lanes)]
        return value, first - start

    def one(device, carry):
        for p in range(pairs):
            slot = device * per_device + 2 * p
            low, low_at = look(slot)
            high, high_at = look(slot + min(1, per_device - 1 - 2 * p))
            low = jnp.where(low_at == 0, low, pltpu.roll(low, embed, 1))
            high = jnp.where(high_at == 0, pltpu.roll(high, embed, 1), high)
            out_ref[device, p] = jnp.where(lane < embed, low, high).astype(out_ref.dtype)
        return carry

    lax.fori_loop(0, devices, one, 0)


def to_slots(table_of, summed, late, embed, devices):
    rows = summed.shape[0]
    per_device = table_of.shape[0] // devices
    pairs = (per_device + 1) // 2
    return pl.pallas_call(
        functools.partial(slot_kernel, embed, per_device),
        out_shape=jax.ShapeDtypeStruct((devices, pairs, rows, 2 * embed), jnp.bfloat16),
        grid_spec=pltpu.PrefetchScalarGridSpec(
            num_scalar_prefetch=1,
            grid=(1,),
            in_specs=[
                pl.BlockSpec(summed.shape, lambda i, s: (0, 0)),
                pl.BlockSpec(late.shape, lambda i, s: (0, 0, 0)),
            ],
            out_specs=pl.BlockSpec((devices, pairs, rows, 2 * embed), lambda i, s: (0, 0, 0, 0)),
            scratch_shapes=[pltpu.VMEM(summed.shape, jnp.float32)],
        ),
        compiler_params=pltpu.CompilerParams(vmem_limit_bytes=32 * 1024 * 1024),
        cost_estimate=pl.CostEstimate(
            flops=4 * rows * summed.shape[1],
            bytes_accessed=10 * rows * summed.shape[1],
            transcendentals=0,
        ),
        name="to_slots",
    )(table_of, summed, late)


def body(
    features,
    cotangent,
    weights,
    biases,
    weight_accum,
    owner_slot,
    bag_ids,
    bag_length,
    tables,
    table_accum,
):
    depth, block_cols, full_width = weights.shape
    data_size = lax.axis_size("dp")
    model_size = lax.axis_size("mp")
    line = model_size // cores
    model_index = lax.axis_index("mp")
    data_index = lax.axis_index("dp")
    spot = model_index // cores
    core = model_index % cores
    first_core = core == 0
    rows = features.shape[0]
    members = data_size // 2
    f32, bf16 = jnp.float32, jnp.bfloat16

    def swap(value):
        return lax.ppermute(value, "mp", [(i, i ^ 1) for i in range(model_size)])

    def hop(value, right, left):
        pairs = [(z * cores, (z + 1) * cores) for z in right]
        pairs += [(z * cores + 1, (z - 1) * cores + 1) for z in left]
        return lax.ppermute(value, "mp", pairs)

    def chip_pair(value):
        other = swap(value)
        return jnp.where(
            first_core,
            jnp.concatenate([value, other], axis=1),
            jnp.concatenate([other, value], axis=1),
        )

    def selected(held, k):
        up, down = held[line - k], held[k]
        if 2 * k == line:
            return up, down
        return jnp.where(first_core, up, down), jnp.where(first_core, down, up)

    def chips(offsets):
        return jnp.stack([(spot + j) % line for j in offsets]).astype(jnp.int32)

    def by_columns(scaled, layer_idx):
        width = cores * block_cols
        held = {}

        def products(offsets, *needed):
            product = column_blocks(
                after(chips(offsets), *needed), scaled, weights, layer_idx, width
            )
            for at, j in enumerate(offsets):
                held[j] = product[at]
            return product

        first = products((1, line - 1))
        rest = lambda sent: (products((*range(2, line - 1), 0), sent),)
        return first, lambda k: selected(held, k), lambda: held[0], rest

    def by_rows(scaled, layer_idx):
        product = row_blocks_product(chips(range(line)), scaled, weights, layer_idx)
        held = [product[j] for j in range(line)]
        return product, lambda k: selected(held, k), lambda: held[0], lambda sent: ()

    def gather_and_reduce(chip, partial, axis, fill, between, complete, reduce_first):
        width = chip.shape[1]
        first, pair, own, rest = partial
        wide = lax.dynamic_update_slice_in_dim(blank((rows, full_width)), chip, spot * width, 1)
        moving = hop(chip, range(0, line - 1), range(1, line))
        moving = after(moving, first)
        inbound, ready = None, None
        if reduce_first:
            mine, theirs = pair(1)
            crossed = after(swap(theirs), *rest(theirs))
            ready = (mine.astype(f32) + crossed.astype(f32)).astype(bf16)
            moving = after(moving, ready)
        for k in range(1, line):
            passed = swap(moving)
            ahead = None
            if k + 1 < line:
                ahead = hop(moving, range(k, line - 1), range(1, line - k))
            for piece, up in ((moving, first_core), (passed, ~first_core)):
                place = jnp.where(up, spot - k, spot + k)
                here = (place >= 0) & (place < line)
                wide = lax.dynamic_update_slice_in_dim(
                    wide, jnp.where(here, piece, chip), jnp.where(here, place, spot) * width, 1
                )
            if k + 1 == line:
                inbound = after(inbound, *complete(wide))
            elif inbound is not None:
                inbound = after(inbound, *between(k, moving))
            if ready is not None:
                total, ready = ready, None
            else:
                mine, theirs = pair(k)
                crossed = swap(theirs)
                total = mine.astype(f32) + crossed.astype(f32)
                if inbound is not None:
                    total = total + inbound.astype(f32)
                total = total.astype(bf16)
            inbound = hop(total, range(k), range(line - k, line))
            if ahead is not None:
                moving = after(ahead, total, *fill(k, total, moving))

        def finish(*needed):
            last = after(inbound, *needed)
            local = own()
            part = local.shape[axis] // cores

            def portion(at):
                return lax.dynamic_slice_in_dim(local, at * part, part, axis).astype(
                    f32
                ) + lax.dynamic_slice_in_dim(last, at * part, part, axis).astype(f32)

            sent = portion(1 - core).astype(bf16)
            return portion(core) + swap(sent).astype(f32)

        return wide, finish

    def crossing(low_core, high_core):
        pairs = []
        for d in range(data_size):
            for m in range(model_size):
                target = (high_core if m % cores else low_core)(d)
                pairs.append((d * model_size + m, target * model_size + m))
        return pairs

    def cross(value, low_core, high_core):
        return lax.ppermute(value, ("dp", "mp"), crossing(low_core, high_core))

    low_flip = lambda d: d ^ 1
    top_flip = lambda d: (d + members) % data_size
    low_turn = lambda k: lambda d: (d // 2 + k) % members * 2 + d % 2
    top_turn = lambda k: lambda d: d // members * members + (d % members + k) % members
    low_bit, low_rest = data_index % 2, data_index // 2
    top_bit, top_rest = data_index // members, data_index % members

    side = core.astype(jnp.int32)
    share = block_cols // data_size
    own_low = (first_core, ~first_core)

    def row_blocks(which, flip):
        turns = jnp.arange(members, dtype=jnp.int32)
        low = (low_rest + turns) % members * 2 + (low_bit ^ flip)
        top = (top_bit ^ flip) * members + (top_rest + turns) % members
        return jnp.where(own_low[which], low, top).astype(jnp.int32)

    sent_index = jnp.concatenate([row_blocks(0, 1), row_blocks(1, 1)])
    grad_index = [
        jnp.concatenate([(side if which == 0 else 1 - side)[None], row_blocks(which, 0)])
        for which in range(2)
    ]
    flips = ((low_flip, top_flip), (top_flip, low_flip))

    def layer_neighbour(wide, *needed):
        sent = column_half(after(side[None], *needed), wide)
        near = cross(sent, *flips[0])
        return (near, swap(near)), sent

    def turned_sums(scaled, *needed):
        turned, own_sent, other_sent = turn(after(sent_index, *needed), scaled, members, share)
        return turned, cross(own_sent, *flips[0]), cross(other_sent, *flips[1])

    def half_sums(which, turned, wide, neighbours, *needed):
        pieces = half_grad(
            after(grad_index[which], *needed),
            turned[0],
            turned[1 + which],
            wide,
            neighbours[which],
        )
        arrived = [pieces[0]]
        for k in range(1, members):
            turns = (low_turn(k), top_turn(k))
            arrived.append(cross(pieces[k], *(turns if which == 0 else turns[::-1])))
        return arrived

    base_f32 = features.astype(f32)
    top_up = cotangent.astype(f32)
    none = lambda k, moving: ()

    def preact_of(wide, layer_idx):
        return forward_product(wide, weights, biases[layer_idx], layer_idx)

    chip = chip_pair(features)
    top_scaled = (after(cotangent, chip).astype(f32) * base_f32).astype(bf16)
    top_turned = []

    def fill_top(k, total, moving):
        if k == 1:
            top_turned.extend(turned_sums(top_scaled, total))
            return (top_turned[0],)
        return ()

    nears = []

    def complete_top(wide):
        near, sent = layer_neighbour(wide)
        nears.append(near)
        return (sent,)

    def complete_low(wide):
        near, sent = layer_neighbour(wide)
        nears.append(near)
        return (sent,)

    first_wide, low_up = gather_and_reduce(
        chip, by_columns(top_scaled, 1), 1, fill_top, none, complete_top, True
    )
    first_pre = preact_of(first_wide, 0)
    current = (base_f32 * first_pre + base_f32).astype(bf16)
    chip = chip_pair(current)
    low_up = top_up + low_up(chip)
    low_scaled = (after(low_up, chip) * base_f32).astype(bf16)
    low_turned, low_sums = [], []

    def fill_low(k, total, moving):
        if k == 1:
            low_turned.extend(turned_sums(low_scaled, moving))
            return (low_turned[0],)
        if k == 2:
            low_half(1, total)
        return ()

    def low_half(which, *needed):
        low_sums.append(half_sums(which, low_turned, first_wide, nears[0], *needed))
        return (low_sums[which][0],)

    def between_low(k, moving):
        return low_half(0, moving) if k == 2 else ()

    second_wide, summed = gather_and_reduce(
        chip, by_rows(low_scaled, 0), 0, fill_low, between_low, complete_low, False
    )
    second_pre = preact_of(second_wide, 1)
    late = (low_up + low_up * first_pre + top_up * second_pre).astype(bf16)
    summed = summed(late)
    late_sent = late
    late = lax.all_to_all(
        late.reshape(model_size, rows // model_size, block_cols),
        "mp",
        split_axis=0,
        concat_axis=0,
        tiled=True,
    )
    tables_all = owner_slot.shape[0]
    embed = full_width // tables_all
    table_of = (
        jnp.zeros((tables_all,), jnp.int32)
        .at[owner_slot]
        .set(jnp.arange(tables_all, dtype=jnp.int32))
    )
    slotted = to_slots(table_of, summed, late, embed, data_size * model_size)
    arrived = lax.all_to_all(slotted, ("dp", "mp"), split_axis=0, concat_axis=0, tiled=True)
    top_sums = [half_sums(which, top_turned, second_wide, nears[1], slotted) for which in range(2)]
    whole, low_accum = weight_update(
        after(side[None], late_sent), weight_accum[0][:, None], *low_sums, 0, depth, None
    )
    arrived = after(arrived, top_sums[0][0], top_sums[1][0], low_accum)

    _, batch, bag = bag_ids.shape
    vocab = tables.shape[1]
    in_bag = jnp.arange(bag, dtype=jnp.int32)[None, None, :] < bag_length[:, :, None]
    ids = jnp.where(in_bag, bag_ids, vocab).transpose(0, 2, 1).reshape(-1)
    new_tables, new_accum = embed_update(
        ids, arrived, jnp.swapaxes(tables, 1, 2), table_accum, bag, batch, learn_rate
    )
    whole, top_accum = weight_update(
        after(side[None], new_accum), weight_accum[1][:, None], *top_sums, 1, depth, whole
    )
    accums = jnp.stack([low_accum[:, 0], top_accum[:, 0]])
    return (whole, accums, jnp.swapaxes(new_tables, 1, 2), new_accum)


def solution(mesh):
    return jax.shard_map(
        body,
        mesh=mesh,
        in_specs=(
            P("dp", "mp"),
            P("dp", "mp"),
            P(None, "mp", None),
            P(None, "mp"),
            P(None, ("mp", "dp")),
            P(),
            P(("dp", "mp"), None, None),
            P(("dp", "mp"), None),
            P(("dp", "mp"), None, None),
            P(("dp", "mp"), None),
        ),
        out_specs=(
            P(None, ("mp", "dp"), None),
            P(None, ("mp", "dp")),
            P(("dp", "mp"), None, None),
            P(("dp", "mp"), None),
        ),
        check_vma=False,
    )
```

profile of v0, /device:TPU:0, one launch (start us, length us, event | category | flops | bytes accessed | tf_op | source)
XLA Modules:
  0.0 430.3 jit_solution(10477128661223667560)
XLA Ops:
  1.3 2.0 collective-permute-done
  3.3 1.9 constant_dynamic-update-slice_fusion.1
  5.5 7.0 %column_blocks.2 = bf16[2,384,2048]{2,1,0:T(8,128)(2,1)S(1)} custom-call(s32[2]{0:T(128)S(1)} %get-tuple-element.114.index_ref, bf16[384,1024]{1,0:T(8,128)(2,1)S(1)} %fusion.2.value_ref, bf16[2,1024,8192]{2,1,0:T(8,128)(2,1)} %weight_ref.7), custom_call_target="tpu_custom_call" | custom-call | flops 3221225472 | bytes 11534336 | tf_op jit(solution)/shard_map/column_blocks/pallas_call | solution.py:208
  13.2 5.8 %collective-permute-start.6 = (bf16[384,2048]{1,0:T(8,128)(2,1)S(1)}, bf16[384,2048]{1,0:T(8,128)(2,1)}, u32[]{:S(2)}, u32[]{:S(2)}) collective-permute-start(bf16[384,2048]{1,0:T(8,128)(2,1)S(1)} %get-tuple-element.99), channel_id=1, source_target_pairs={{0,2},{2,4},{4,6},{3,1},{5,3},{7,5},{8,10},{10,12},{12,14},{11,9},... | collective-permute-start | bytes 4718600 | tf_op jit(solution)/shard_map/ppermute | solution.py:457
  18.9 7.0 %column_blocks.3 = bf16[2,384,2048]{2,1,0:T(8,128)(2,1)S(1)} custom-call(s32[2]{0:T(128)S(1)} %get-tuple-element.50.index_ref, bf16[384,1024]{1,0:T(8,128)(2,1)S(1)} %fusion.2.value_ref, bf16[2,1024,8192]{2,1,0:T(8,128)(2,1)} %weight_ref.7), custom_call_target="tpu_custom_call" | custom-call | flops 3221225472 | bytes 11534336 | tf_op jit(solution)/shard_map/column_blocks/pallas_call | solution.py:208
  26.0 2.7 add_convert_fusion.5
  28.6 7.0 %collective-permute-done.6 = bf16[384,2048]{1,0:T(8,128)(2,1)} collective-permute-done((bf16[384,2048]{1,0:T(8,128)(2,1)S(1)}, bf16[384,2048]{1,0:T(8,128)(2,1)}, u32[]{:S(2)}, u32[]{:S(2)}) %collective-permute-start.6) | collective-permute-done | bytes 1572896 | tf_op jit(solution)/shard_map/ppermute | solution.py:457
  35.7 2.0 collective-permute-start.8
  37.7 8.5 %collective-permute-start.4 = (bf16[384,2048]{1,0:T(8,128)(2,1)}, bf16[384,2048]{1,0:T(8,128)(2,1)}, u32[]{:S(2)}, u32[]{:S(2)}) collective-permute-start(bf16[384,2048]{1,0:T(8,128)(2,1)} %get-tuple-element.100), channel_id=1, source_target_pairs={{0,2},{7,5},{8,10},{15,13},{16,18},{23,21},{24,26},{31,29}} | collective-permute-start | bytes 4718600 | tf_op jit(solution)/shard_map/ppermute | solution.py:457
  46.2 2.0 fusion.15
  53.4 3.4 select_dynamic-update-slice_fusion.11
  56.8 6.5 %collective-permute-done.4 = bf16[384,2048]{1,0:T(8,128)(2,1)} collective-permute-done((bf16[384,2048]{1,0:T(8,128)(2,1)}, bf16[384,2048]{1,0:T(8,128)(2,1)}, u32[]{:S(2)}, u32[]{:S(2)}) %collective-permute-start.4) | collective-permute-done | bytes 1572896 | tf_op jit(solution)/shard_map/ppermute | solution.py:457
  63.2 3.9 add_convert_fusion.4
  67.1 5.5 %collective-permute-start.5 = (bf16[384,2048]{1,0:T(8,128)(2,1)}, bf16[384,2048]{1,0:T(8,128)(2,1)}, u32[]{:S(2)}, u32[]{:S(2)}) collective-permute-start(bf16[384,2048]{1,0:T(8,128)(2,1)} %add_convert_fusion.4), channel_id=1, source_target_pairs={{0,2},{2,4},{5,3},{7,5},{8,10},{10,12},{13,11},{15,13},{16,18},{18... | collective-permute-start | bytes 4718600 | tf_op jit(solution)/shard_map/ppermute | solution.py:457
  72.6 1.8 select_dynamic-update-slice_fusion.10
  74.4 4.6 %collective-permute-start.11 = (bf16[384,2048]{1,0:T(8,128)(2,1)S(1)}, bf16[384,2048]{1,0:T(8,128)(2,1)S(1)}, u32[]{:S(2)}, u32[]{:S(2)}) collective-permute-start(bf16[384,2048]{1,0:T(8,128)(2,1)S(1)} %collective-permute-done.10), channel_id=1, source_target_pairs={{0,1},{1,0},{2,3},{3,2},{4,5},{5,4},{6,7},{7,6},{8,9},{9,8},{10,11... | collective-permute-start | bytes 4718600 | tf_op jit(solution)/shard_map/ppermute | solution.py:452
  79.0 1.8 select_dynamic-update-slice_fusion.9
  80.8 1.8 select_dynamic-update-slice_fusion.8
  82.5 1.8 select_dynamic-update-slice_fusion.7
  84.3 1.8 select_dynamic-update-slice_fusion.6.value_ref.wide_ref.refs_3_
  86.0 4.2 column_half.2
  90.3 4.2 add_convert_fusion.3
  94.5 6.5 %collective-permute-start.12 = (bf16[384,2048]{1,0:T(8,128)(2,1)}, bf16[384,2048]{1,0:T(8,128)(2,1)}, u32[]{:S(2)}, u32[]{:S(2)}) collective-permute-start(bf16[384,2048]{1,0:T(8,128)(2,1)} %add_convert_fusion.3), channel_id=1, source_target_pairs={{0,2},{2,4},{4,6},{3,1},{5,3},{7,5},{8,10},{10,12},{12,14},{11,9},... | collective-permute-start | bytes 4718600 | tf_op jit(solution)/shard_map/ppermute | solution.py:457
  101.0 13.2 %forward_product.2 = f32[384,1024]{1,0:T(8,128)S(1)} custom-call(bf16[384,8192]{1,0:T(8,128)(2,1)} %select_dynamic-update-slice_fusion.6.value_ref.wide_ref.refs_3_, bf16[2,1024,8192]{2,1,0:T(8,128)(2,1)} %weight_ref.7, f32[1,1024]{1,0:T(1,128)S(1)} %get-tuple-element.108.bias_ref), custom_call_target="tpu_custom_call" | custom-call | flops 6442450944 | bytes 23068672 | tf_op jit(solution)/shard_map/forward_product/pallas_call | solution.py:284
  114.6 2.2 collective-permute-done.13
  116.8 2.4 constant_dynamic-update-slice_fusion
  119.2 2.4 fusion.7
  121.9 5.5 %collective-permute-start.19 = (bf16[384,2048]{1,0:T(8,128)(2,1)}, bf16[384,2048]{1,0:T(8,128)(2,1)}, u32[]{:S(2)}, u32[]{:S(2)}) collective-permute-start(bf16[384,2048]{1,0:T(8,128)(2,1)} %get-tuple-element.95), channel_id=1, source_target_pairs={{0,2},{2,4},{4,6},{3,1},{5,3},{7,5},{8,10},{10,12},{12,14},{11,9},... | collective-permute-start | bytes 4718600 | tf_op jit(solution)/shard_map/ppermute | solution.py:457
  127.4 2.2 convert_add_fusion.1
  131.0 12.4 %row_blocks_product.1 = bf16[4,96,8192]{2,1,0:T(8,128)(2,1)S(1)} custom-call(s32[4]{0:T(128)S(1)} %pad_add_fusion.index_ref, bf16[384,1024]{1,0:T(8,128)(2,1)S(1)} %fusion.4.refs_0_.refs_1_.refs_2_.refs_3_.value_ref, bf16[384,1024]{1,0:T(8,128)(2,1)S(1)} %fusion.4.refs_0_.refs_1_.refs_2_.refs_3_.value_ref, ...), custom_call_target="tpu_custom_call" | custom-call | flops 6442450944 | bytes 23068672 | tf_op jit(solution)/shard_map/row_blocks_product/pallas_call | solution.py:247
  143.4 2.4 fusion.14
  145.8 1.8 copy-done
  151.3 4.5 %add_convert_fusion.2 = (bf16[96,8192]{1,0:T(8,128)(2,1)S(1)}, bf16[96,8192]{1,0:T(8,128)(2,1)}) fusion(bf16[96,8192]{1,0:T(8,128)(2,1)} %collective-permute-done.17, bf16[4,96,8192]{2,1,0:T(8,128)(2,1)} %copy-done, pred[]{:T(512)S(6)} %eq.24), kind=kLoop, calls=%fused_computation.3 | loop fusion | flops 3932160 | bytes 7864321 | tf_op jit(solution)/shard_map/convert_element_type | solution.py:532
  155.8 5.6 %collective-permute-start.18 = (bf16[96,8192]{1,0:T(8,128)(2,1)S(1)}, bf16[96,8192]{1,0:T(8,128)(2,1)S(1)}, u32[]{:S(2)}, u32[]{:S(2)}) collective-permute-start(bf16[96,8192]{1,0:T(8,128)(2,1)S(1)} %get-tuple-element.96), channel_id=1, source_target_pairs={{0,2},{7,5},{8,10},{15,13},{16,18},{23,21},{24,26},{31,29}} | collective-permute-start | bytes 4718600 | tf_op jit(solution)/shard_map/ppermute | solution.py:457
  162.4 22.7 %collective-permute-done.22.refs_4_ = bf16[384,4096]{1,0:T(8,128)(2,1)} collective-permute-done((bf16[384,4096]{1,0:T(8,128)(2,1)}, bf16[384,4096]{1,0:T(8,128)(2,1)}, u32[]{:S(2)}, u32[]{:S(2)}) %collective-permute-start.22) | collective-permute-done | bytes 3145760 | tf_op jit(solution)/shard_map/ppermute | solution.py:561
  186.6 1.8 select_dynamic-update-slice_fusion.5
  189.3 3.6 collective-permute-done.21.refs_2_
  193.7 8.2 %half_grad.4 = (bf16[256,4096]{1,0:T(8,128)(2,1)S(1)}, bf16[256,4096]{1,0:T(8,128)(2,1)}) custom-call(s32[3]{0:T(128)S(1)} %pad_add_fusion.4.index_ref, bf16[1024,384]{1,0:T(8,128)(2,1)S(1)} %get-tuple-element.63.refs_0_.refs_1_, bf16[1024,384]{1,0:T(8,128)(2,1)S(1)} %get-tuple-element.63.refs_0_.refs_1_, ...), custom_call_target="tpu_custom_call" | custom-call | flops 3221225472 | bytes 10485760 | tf_op jit(solution)/shard_map/half_grad/pallas_call | solution.py:149
  201.9 1.8 select_dynamic-update-slice_fusion.4
  204.3 3.1 add_convert_fusion.1
  207.4 5.4 %collective-permute-start.27 = (bf16[384,2048]{1,0:T(8,128)(2,1)S(1)}, bf16[384,2048]{1,0:T(8,128)(2,1)S(1)}, u32[]{:S(2)}, u32[]{:S(2)}) collective-permute-start(bf16[384,2048]{1,0:T(8,128)(2,1)S(1)} %collective-permute-done.26), channel_id=1, source_target_pairs={{0,1},{1,0},{2,3},{3,2},{4,5},{5,4},{6,7},{7,6},{8,9},{9,8},{10,11... | collective-permute-start | bytes 4718600 | tf_op jit(solution)/shard_map/ppermute | solution.py:452
  212.9 1.8 select_dynamic-update-slice_fusion.3
  214.7 2.9 collective-permute-start.23
  217.6 1.7 select_dynamic-update-slice_fusion.2
  219.3 1.8 select_dynamic-update-slice_fusion.1
  221.1 1.8 select_dynamic-update-slice_fusion.value_ref.wide_ref.refs_3_
  222.9 4.2 column_half.3
  228.6 6.0 %collective-permute-done.23 = bf16[96,8192]{1,0:T(8,128)(2,1)} collective-permute-done((bf16[96,8192]{1,0:T(8,128)(2,1)}, bf16[96,8192]{1,0:T(8,128)(2,1)}, u32[]{:S(2)}, u32[]{:S(2)}) %collective-permute-start.23) | collective-permute-done | bytes 1572896 | tf_op jit(solution)/shard_map/ppermute | solution.py:457
  234.6 4.2 add_convert_fusion
  238.8 7.6 %collective-permute-start.28 = (bf16[96,8192]{1,0:T(8,128)(2,1)}, bf16[96,8192]{1,0:T(8,128)(2,1)}, u32[]{:S(2)}, u32[]{:S(2)}) collective-permute-start(bf16[96,8192]{1,0:T(8,128)(2,1)} %add_convert_fusion), channel_id=1, source_target_pairs={{0,2},{2,4},{4,6},{3,1},{5,3},{7,5},{8,10},{10,12},{12,14},{11,9},... | collective-permute-start | bytes 4718600 | tf_op jit(solution)/shard_map/ppermute | solution.py:457
  246.5 13.3 %forward_product.3 = f32[384,1024]{1,0:T(8,128)S(1)} custom-call(bf16[384,8192]{1,0:T(8,128)(2,1)} %select_dynamic-update-slice_fusion.value_ref.wide_ref.refs_3_, bf16[2,1024,8192]{2,1,0:T(8,128)(2,1)} %weight_ref.7, f32[1,1024]{1,0:T(1,128)S(1)} %get-tuple-element.107.bias_ref), custom_call_target="tpu_custom_call" | custom-call | flops 6442450944 | bytes 23068672 | tf_op jit(solution)/shard_map/forward_product/pallas_call | solution.py:284
  261.3 2.2 collective-permute-done.28
  269.7 4.7 %collective-permute-done.35.refs_2_ = bf16[2,256,384]{2,1,0:T(8,128)(2,1)S(1)} collective-permute-done((bf16[2,256,384]{2,1,0:T(8,128)(2,1)S(1)}, bf16[2,256,384]{2,1,0:T(8,128)(2,1)S(1)}, u32[]{:S(2)}, u32[]{:S(2)}) %collective-permute-start.35) | collective-permute-done | bytes 393248 | tf_op jit(solution)/shard_map/ppermute | solution.py:561
  277.4 8.3 %half_grad.7 = (bf16[256,4096]{1,0:T(8,128)(2,1)S(1)}, bf16[256,4096]{1,0:T(8,128)(2,1)}) custom-call(s32[3]{0:T(128)S(1)} %pad_add_fusion.5.index_ref, bf16[1024,384]{1,0:T(8,128)(2,1)S(1)} %copy-done.16, bf16[1024,384]{1,0:T(8,128)(2,1)S(1)} %copy-done.16, bf16[2,256,384]{2,1,0:T(8,128)(2,1)S(1)} %collective-permute-done.35.refs_2_, ...), custom_call_target="tpu_custom_call" | custom-call | flops 3221225472 | bytes 10485760 | tf_op jit(solution)/shard_map/half_grad/pallas_call | solution.py:149
  287.0 5.9 %all-to-all-start = ((bf16[8,48,1024]{2,1,0:T(8,128)(2,1)}), bf16[8,48,1024]{2,1,0:T(8,128)(2,1)S(1)}, u32[]{:S(2)}, u32[]{:S(2)}) async-start(bf16[8,48,1024]{2,1,0:T(8,128)(2,1)} %bitcast.16), calls=%async_computation | async-start | bytes 1572864 | tf_op jit(solution)/shard_map/all_to_all | solution.py:671
  295.2 18.7 %all-to-all-done.late_ref = bf16[8,48,1024]{2,1,0:T(8,128)(2,1)S(1)} async-done(((bf16[8,48,1024]{2,1,0:T(8,128)(2,1)}), bf16[8,48,1024]{2,1,0:T(8,128)(2,1)S(1)}, u32[]{:S(2)}, u32[]{:S(2)}) %all-to-all-start) | async-done | bytes 786464 | tf_op jit(solution)/shard_map/all_to_all | solution.py:671
  313.9 4.8 %to_slots.1 = bf16[32,2,48,128]{3,2,1,0:T(8,128)(2,1)} custom-call(s32[128]{0:T(128)S(1)} %scatter_custom_fusion.table_ref, f32[48,8192]{1,0:T(8,128)S(1)} %fusion.6.summed_ref, bf16[8,48,1024]{2,1,0:T(8,128)(2,1)S(1)} %all-to-all-done.late_ref), custom_call_target="tpu_custom_call" | custom-call | flops 1572864 | bytes 3932160 | tf_op jit(solution)/shard_map/to_slots/pallas_call | solution.py:403
  318.7 8.4 %half_grad.5 = (bf16[256,4096]{1,0:T(8,128)(2,1)S(1)}, bf16[256,4096]{1,0:T(8,128)(2,1)}) custom-call(s32[3]{0:T(128)S(1)} %pad_add_fusion.4.index_ref, bf16[1024,384]{1,0:T(8,128)(2,1)S(1)} %copy-done.14, bf16[1024,384]{1,0:T(8,128)(2,1)S(1)} %copy-done.14, bf16[2,256,384]{2,1,0:T(8,128)(2,1)} %collective-permute-done.30.refs_2_, ...), custom_call_target="tpu_custom_call" | custom-call | flops 3221225472 | bytes 10485760 | tf_op jit(solution)/shard_map/half_grad/pallas_call | solution.py:149
  328.9 8.4 %half_grad.6 = (bf16[256,4096]{1,0:T(8,128)(2,1)S(1)}, bf16[256,4096]{1,0:T(8,128)(2,1)}) custom-call(s32[3]{0:T(128)S(1)} %pad_add_fusion.5.index_ref, bf16[1024,384]{1,0:T(8,128)(2,1)S(1)} %copy-done.14, bf16[1024,384]{1,0:T(8,128)(2,1)S(1)} %copy-done.14, bf16[2,256,384]{2,1,0:T(8,128)(2,1)} %collective-permute-done.32.refs_2_, ...), custom_call_target="tpu_custom_call" | custom-call | flops 3221225472 | bytes 10485760 | tf_op jit(solution)/shard_map/half_grad/pallas_call | solution.py:149
  339.2 3.5 all-to-all-start.1
  345.4 8.5 %weight_update.2 = (f32[2,256,8192]{2,1,0:T(8,128)}, f32[256,1]{1,0:T(8,128)S(1)}) custom-call(s32[1]{0:T(128)} %bitcast.index_ref.side_ref, f32[256,1]{1,0:T(8,128)S(1)} %copy.15.accum_ref, bf16[256,4096]{1,0:T(8,128)(2,1)S(1)} %copy-done.6, bf16[256,4096]{1,0:T(8,128)(2,1)} %collective-permute-done.34.refs_1_, bf16[256,4096]{1,0:T(8,128)(2,1)S(1)} %copy-done.8, ...), custom_call_target="tpu_custom_call" | custom-call | flops 8388608 | bytes 16777216 | tf_op jit(solution)/shard_map/weight_update/pallas_call | solution.py:346
  354.1 31.2 %all-to-all-done.1.g_ref = bf16[32,2,48,128]{3,2,1,0:T(8,128)(2,1)S(1)} async-done(((bf16[32,2,48,128]{3,2,1,0:T(8,128)(2,1)}), bf16[32,2,48,128]{3,2,1,0:T(8,128)(2,1)S(1)}, u32[]{:S(2)}, u32[]{:S(2)}) %all-to-all-start.1) | async-done | bytes 786464 | tf_op jit(solution)/shard_map/all_to_all | solution.py:686
  386.2 34.8 %embed_update.1 = (f32[4,64,8192]{2,1,0:T(8,128)}, f32[4,8192]{1,0:T(4,128)}) custom-call(s32[24576]{0:T(1024)} %reshape.35.ids_ref, bf16[32,2,48,128]{3,2,1,0:T(8,128)(2,1)} %copy-done.32, f32[4,64,8192]{2,1,0:T(8,128)} %bitcast.49, f32[4,8192]{1,0:T(4,128)} %acc_in_ref.1), custom_call_target="tpu_custom_call" | custom-call | flops 100000000 | bytes 150000000 | tf_op jit(solution)/shard_map/embed_update/pallas_call | solution.py:64
  421.0 8.5 %weight_update.3 = (f32[2,256,8192]{2,1,0:T(8,128)}, f32[256,1]{1,0:T(8,128)S(1)}) custom-call(s32[1]{0:T(128)} %bitcast.index_ref.side_ref, f32[256,1]{1,0:T(8,128)S(1)} %copy.16.accum_ref, bf16[256,4096]{1,0:T(8,128)(2,1)S(1)} %copy-done.10, bf16[256,4096]{1,0:T(8,128)(2,1)} %collective-permute-done.38.refs_1_, ...), custom_call_target="tpu_custom_call", output_to_operand_aliasing={{0}: (6, {})} | custom-call | flops 8388608 | bytes 16777216 | tf_op jit(solution)/shard_map/weight_update/pallas_call | solution.py:346
  (166 shorter events, 40.9 us)
Async XLA Ops:
  0.6 2.7 collective-permute-start
  5.2 7.9 %copy-start.19 = (bf16[384,2048]{1,0:T(8,128)(2,1)}, bf16[384,2048]{1,0:T(8,128)(2,1)S(1)}, u32[]{:S(2)}) copy-start(bf16[384,2048]{1,0:T(8,128)(2,1)S(1)} %get-tuple-element.99) | copy-start | bytes 4718596
  5.5 13.4 %copy-start.3 = (bf16[384,1024]{1,0:T(8,128)(2,1)}, bf16[384,1024]{1,0:T(8,128)(2,1)S(1)}, u32[]{:S(2)}) copy-start(bf16[384,1024]{1,0:T(8,128)(2,1)S(1)} %fusion.2.value_ref) | copy-start | bytes 2359300
  12.7 13.2 %collective-permute-start.3 = (bf16[384,2048]{1,0:T(8,128)(2,1)S(1)}, bf16[384,2048]{1,0:T(8,128)(2,1)S(1)}, u32[]{:S(2)}, u32[]{:S(2)}) collective-permute-start(bf16[384,2048]{1,0:T(8,128)(2,1)S(1)} %select_bitcast_fusion.3), channel_id=1, source_target_pairs={{0,1},{1,0},{2,3},{3,2},{4,5},{5,4},{6,7},{7,6},{8,9},{9,8},{10,11... | collective-permute-start | bytes 4718600 | tf_op jit(solution)/shard_map/ppermute | solution.py:452
  13.2 22.5 %collective-permute-start.6 = (bf16[384,2048]{1,0:T(8,128)(2,1)S(1)}, bf16[384,2048]{1,0:T(8,128)(2,1)}, u32[]{:S(2)}, u32[]{:S(2)}) collective-permute-start(bf16[384,2048]{1,0:T(8,128)(2,1)S(1)} %get-tuple-element.99), channel_id=1, source_target_pairs={{0,2},{2,4},{4,6},{3,1},{5,3},{7,5},{8,10},{10,12},{12,14},{11,9},... | collective-permute-start | bytes 4718600 | tf_op jit(solution)/shard_map/ppermute | solution.py:457
  25.9 20.3 %copy-start.1 = (bf16[2,384,2048]{2,1,0:T(8,128)(2,1)}, bf16[2,384,2048]{2,1,0:T(8,128)(2,1)S(1)}, u32[]{:S(2)}) copy-start(bf16[2,384,2048]{2,1,0:T(8,128)(2,1)S(1)} %column_blocks.3) | copy-start | bytes 9437188
  35.7 13.2 %copy-start.35 = (f32[2,1024]{1,0:T(2,128)S(1)}, f32[2,1024]{1,0:T(2,128)}, u32[]{:S(2)}) copy-start(f32[2,1024]{1,0:T(2,128)} %param.13) | copy-start | bytes 24580
  35.7 16.9 %collective-permute-start.8 = (bf16[384,2048]{1,0:T(8,128)(2,1)}, bf16[384,2048]{1,0:T(8,128)(2,1)}, u32[]{:S(2)}, u32[]{:S(2)}) collective-permute-start(bf16[384,2048]{1,0:T(8,128)(2,1)} %collective-permute-done.6), channel_id=1, source_target_pairs={{2,4},{4,6},{3,1},{5,3},{10,12},{12,14},{11,9},{13,11},{18,20},{20... | collective-permute-start | bytes 4718600 | tf_op jit(solution)/shard_map/ppermute | solution.py:457
  37.7 25.5 %collective-permute-start.4 = (bf16[384,2048]{1,0:T(8,128)(2,1)}, bf16[384,2048]{1,0:T(8,128)(2,1)}, u32[]{:S(2)}, u32[]{:S(2)}) collective-permute-start(bf16[384,2048]{1,0:T(8,128)(2,1)} %get-tuple-element.100), channel_id=1, source_target_pairs={{0,2},{7,5},{8,10},{15,13},{16,18},{23,21},{24,26},{31,29}} | collective-permute-start | bytes 4718600 | tf_op jit(solution)/shard_map/ppermute | solution.py:457
  48.2 15.0 %collective-permute-start.2 = (bf16[384,2048]{1,0:T(8,128)(2,1)}, bf16[384,2048]{1,0:T(8,128)(2,1)}, u32[]{:S(2)}, u32[]{:S(2)}) collective-permute-start(bf16[384,2048]{1,0:T(8,128)(2,1)} %get-tuple-element.106), channel_id=1, source_target_pairs={{0,1},{1,0},{2,3},{3,2},{4,5},{5,4},{6,7},{7,6},{8,9},{9,8},{10,11... | collective-permute-start | bytes 4718600 | tf_op jit(solution)/shard_map/ppermute | solution.py:452
  48.2 24.4 %collective-permute-start.7 = (bf16[384,2048]{1,0:T(8,128)(2,1)}, bf16[384,2048]{1,0:T(8,128)(2,1)S(1)}, u32[]{:S(2)}, u32[]{:S(2)}) collective-permute-start(bf16[384,2048]{1,0:T(8,128)(2,1)} %collective-permute-done.6), channel_id=1, source_target_pairs={{0,1},{1,0},{2,3},{3,2},{4,5},{5,4},{6,7},{7,6},{8,9},{9,8},{10,11... | collective-permute-start | bytes 4718600 | tf_op jit(solution)/shard_map/ppermute | solution.py:452
  52.6 37.7 %collective-permute-start.1 = (bf16[384,2048]{1,0:T(8,128)(2,1)}, bf16[384,2048]{1,0:T(8,128)(2,1)}, u32[]{:S(2)}, u32[]{:S(2)}) collective-permute-start(bf16[384,2048]{1,0:T(8,128)(2,1)} %get-tuple-element.101), channel_id=1, source_target_pairs={{0,1},{1,0},{2,3},{3,2},{4,5},{5,4},{6,7},{7,6},{8,9},{9,8},{10,11... | collective-permute-start | bytes 4718600 | tf_op jit(solution)/shard_map/ppermute | solution.py:452
  52.6 21.8 %collective-permute-start.10 = (bf16[384,2048]{1,0:T(8,128)(2,1)}, bf16[384,2048]{1,0:T(8,128)(2,1)S(1)}, u32[]{:S(2)}, u32[]{:S(2)}) collective-permute-start(bf16[384,2048]{1,0:T(8,128)(2,1)} %collective-permute-done.8), channel_id=1, source_target_pairs={{4,6},{3,1},{12,14},{11,9},{20,22},{19,17},{28,30},{27,25}} | collective-permute-start | bytes 4718600 | tf_op jit(solution)/shard_map/ppermute | solution.py:457
  53.3 9.9 %copy-start.2 = (bf16[2,384,2048]{2,1,0:T(8,128)(2,1)S(1)}, bf16[2,384,2048]{2,1,0:T(8,128)(2,1)}, u32[]{:S(2)}) copy-start(bf16[2,384,2048]{2,1,0:T(8,128)(2,1)} %copy-done.1) | copy-start | bytes 9437188
  56.8 15.9 %copy-start.20 = (bf16[384,2048]{1,0:T(8,128)(2,1)S(1)}, bf16[384,2048]{1,0:T(8,128)(2,1)}, u32[]{:S(2)}) copy-start(bf16[384,2048]{1,0:T(8,128)(2,1)} %copy-done.19) | copy-start | bytes 4718596
  63.2 17.5 %collective-permute-start.9 = (bf16[384,2048]{1,0:T(8,128)(2,1)}, bf16[384,2048]{1,0:T(8,128)(2,1)S(1)}, u32[]{:S(2)}, u32[]{:S(2)}) collective-permute-start(bf16[384,2048]{1,0:T(8,128)(2,1)} %collective-permute-done.8), channel_id=1, source_target_pairs={{0,1},{1,0},{2,3},{3,2},{4,5},{5,4},{6,7},{7,6},{8,9},{9,8},{10,11... | collective-permute-start | bytes 4718600 | tf_op jit(solution)/shard_map/ppermute | solution.py:452
  67.1 23.1 %collective-permute-start.5 = (bf16[384,2048]{1,0:T(8,128)(2,1)}, bf16[384,2048]{1,0:T(8,128)(2,1)}, u32[]{:S(2)}, u32[]{:S(2)}) collective-permute-start(bf16[384,2048]{1,0:T(8,128)(2,1)} %add_convert_fusion.4), channel_id=1, source_target_pairs={{0,2},{2,4},{5,3},{7,5},{8,10},{10,12},{13,11},{15,13},{16,18},{18... | collective-permute-start | bytes 4718600 | tf_op jit(solution)/shard_map/ppermute | solution.py:457
  74.4 9.9 %collective-permute-start.11 = (bf16[384,2048]{1,0:T(8,128)(2,1)S(1)}, bf16[384,2048]{1,0:T(8,128)(2,1)S(1)}, u32[]{:S(2)}, u32[]{:S(2)}) collective-permute-start(bf16[384,2048]{1,0:T(8,128)(2,1)S(1)} %collective-permute-done.10), channel_id=1, source_target_pairs={{0,1},{1,0},{2,3},{3,2},{4,5},{5,4},{6,7},{7,6},{8,9},{9,8},{10,11... | collective-permute-start | bytes 4718600 | tf_op jit(solution)/shard_map/ppermute | solution.py:452
  94.5 24.8 %collective-permute-start.12 = (bf16[384,2048]{1,0:T(8,128)(2,1)}, bf16[384,2048]{1,0:T(8,128)(2,1)}, u32[]{:S(2)}, u32[]{:S(2)}) collective-permute-start(bf16[384,2048]{1,0:T(8,128)(2,1)} %add_convert_fusion.3), channel_id=1, source_target_pairs={{0,2},{2,4},{4,6},{3,1},{5,3},{7,5},{8,10},{10,12},{12,14},{11,9},... | collective-permute-start | bytes 4718600 | tf_op jit(solution)/shard_map/ppermute | solution.py:457
  101.0 13.2 %copy-start.25 = (bf16[384,1024]{1,0:T(8,128)(2,1)S(1)}, bf16[384,1024]{1,0:T(8,128)(2,1)}, u32[]{:S(2)}) copy-start(bf16[384,1024]{1,0:T(8,128)(2,1)} %param.10) | copy-start | bytes 2359300
  114.5 2.4 collective-permute-start.13
  119.2 8.1 %copy-start.28 = (bf16[384,1024]{1,0:T(8,128)(2,1)S(1)}, bf16[384,1024]{1,0:T(8,128)(2,1)}, u32[]{:S(2)}) copy-start(bf16[384,1024]{1,0:T(8,128)(2,1)} %param.11) | copy-start | bytes 2359300
  121.7 5.7 %collective-permute-start.14 = (bf16[384,1024]{1,0:T(8,128)(2,1)}, bf16[384,1024]{1,0:T(8,128)(2,1)}, u32[]{:S(2)}, u32[]{:S(2)}) collective-permute-start(bf16[384,1024]{1,0:T(8,128)(2,1)} %fusion.7), channel_id=1, source_target_pairs={{0,1},{1,0},{2,3},{3,2},{4,5},{5,4},{6,7},{7,6},{8,9},{9,8},{10,11... | collective-permute-start | bytes 2359304 | tf_op jit(solution)/shard_map/ppermute | solution.py:452
  121.9 8.8 %copy-start.26 = (bf16[384,1024]{1,0:T(8,128)(2,1)S(1)}, bf16[384,1024]{1,0:T(8,128)(2,1)}, u32[]{:S(2)}) copy-start(bf16[384,1024]{1,0:T(8,128)(2,1)} %param.10) | copy-start | bytes 2359300
  121.9 27.1 %collective-permute-start.19 = (bf16[384,2048]{1,0:T(8,128)(2,1)}, bf16[384,2048]{1,0:T(8,128)(2,1)}, u32[]{:S(2)}, u32[]{:S(2)}) collective-permute-start(bf16[384,2048]{1,0:T(8,128)(2,1)} %get-tuple-element.95), channel_id=1, source_target_pairs={{0,2},{2,4},{4,6},{3,1},{5,3},{7,5},{8,10},{10,12},{12,14},{11,9},... | collective-permute-start | bytes 4718600 | tf_op jit(solution)/shard_map/ppermute | solution.py:457
  147.5 3.8 collective-permute-start.17
  147.5 37.6 %collective-permute-start.22 = (bf16[384,4096]{1,0:T(8,128)(2,1)}, bf16[384,4096]{1,0:T(8,128)(2,1)}, u32[]{:S(2)}, u32[]{:S(2)}) collective-permute-start(bf16[384,4096]{1,0:T(8,128)(2,1)} %column_half.2), channel_id=1, source_target_pairs={{0,8},{1,17},{2,10},{3,19},{4,12},{5,21},{6,14},{7,23},{8,0},{9,25... | collective-permute-start | bytes 9437192 | tf_op jit(solution)/shard_map/ppermute | solution.py:561
  149.0 39.4 %collective-permute-start.20 = (bf16[384,2048]{1,0:T(8,128)(2,1)}, bf16[384,2048]{1,0:T(8,128)(2,1)S(1)}, u32[]{:S(2)}, u32[]{:S(2)}) collective-permute-start(bf16[384,2048]{1,0:T(8,128)(2,1)} %collective-permute-done.19), channel_id=1, source_target_pairs={{2,4},{4,6},{3,1},{5,3},{10,12},{12,14},{11,9},{13,11},{18,20},{20... | collective-permute-start | bytes 4718600 | tf_op jit(solution)/shard_map/ppermute | solution.py:457
  149.8 52.1 %collective-permute-start.24 = (bf16[384,2048]{1,0:T(8,128)(2,1)}, bf16[384,2048]{1,0:T(8,128)(2,1)S(1)}, u32[]{:S(2)}, u32[]{:S(2)}) collective-permute-start(bf16[384,2048]{1,0:T(8,128)(2,1)} %collective-permute-done.19), channel_id=1, source_target_pairs={{0,1},{1,0},{2,3},{3,2},{4,5},{5,4},{6,7},{7,6},{8,9},{9,8},{10,11... | collective-permute-start | bytes 4718600 | tf_op jit(solution)/shard_map/ppermute | solution.py:452
  150.6 53.6 %collective-permute-start.16 = (bf16[96,8192]{1,0:T(8,128)(2,1)}, bf16[96,8192]{1,0:T(8,128)(2,1)S(1)}, u32[]{:S(2)}, u32[]{:S(2)}) collective-permute-start(bf16[96,8192]{1,0:T(8,128)(2,1)} %get-tuple-element.103), channel_id=1, source_target_pairs={{0,1},{1,0},{2,3},{3,2},{4,5},{5,4},{6,7},{7,6},{8,9},{9,8},{10,11... | collective-permute-start | bytes 4718600 | tf_op jit(solution)/shard_map/ppermute | solution.py:452
  151.3 35.3 %copy-start.21 = (bf16[384,2048]{1,0:T(8,128)(2,1)S(1)}, bf16[384,2048]{1,0:T(8,128)(2,1)}, u32[]{:S(2)}) copy-start(bf16[384,2048]{1,0:T(8,128)(2,1)} %get-tuple-element.95) | copy-start | bytes 4718596
  155.8 48.0 %collective-permute-start.18 = (bf16[96,8192]{1,0:T(8,128)(2,1)S(1)}, bf16[96,8192]{1,0:T(8,128)(2,1)S(1)}, u32[]{:S(2)}, u32[]{:S(2)}) collective-permute-start(bf16[96,8192]{1,0:T(8,128)(2,1)S(1)} %get-tuple-element.96), channel_id=1, source_target_pairs={{0,2},{7,5},{8,10},{15,13},{16,18},{23,21},{24,26},{31,29}} | collective-permute-start | bytes 4718600 | tf_op jit(solution)/shard_map/ppermute | solution.py:457
  162.4 26.0 %copy-start.17 = (bf16[2,256,384]{2,1,0:T(8,128)(2,1)}, bf16[2,256,384]{2,1,0:T(8,128)(2,1)S(1)}, u32[]{:S(2)}) copy-start(bf16[2,256,384]{2,1,0:T(8,128)(2,1)S(1)} %get-tuple-element.81) | copy-start | bytes 1179652
  162.4 31.3 %copy-start.15 = (bf16[1024,384]{1,0:T(8,128)(2,1)}, bf16[1024,384]{1,0:T(8,128)(2,1)S(1)}, u32[]{:S(2)}) copy-start(bf16[1024,384]{1,0:T(8,128)(2,1)S(1)} %get-tuple-element.63.refs_0_.refs_1_) | copy-start | bytes 2359300
  185.1 7.8 %collective-permute-start.21 = (bf16[2,256,384]{2,1,0:T(8,128)(2,1)S(1)}, bf16[2,256,384]{2,1,0:T(8,128)(2,1)S(1)}, u32[]{:S(2)}, u32[]{:S(2)}) collective-permute-start(bf16[2,256,384]{2,1,0:T(8,128)(2,1)S(1)} %get-tuple-element.66), channel_id=1, source_target_pairs={{0,8},{1,17},{2,10},{3,19},{4,12},{5,21},{6,14},{7,23},{8,0},{9,25... | collective-permute-start | bytes 1179656 | tf_op jit(solution)/shard_map/ppermute | solution.py:561
  188.4 87.4 %collective-permute-start.36 = (bf16[384,4096]{1,0:T(8,128)(2,1)}, bf16[384,4096]{1,0:T(8,128)(2,1)}, u32[]{:S(2)}, u32[]{:S(2)}) collective-permute-start(bf16[384,4096]{1,0:T(8,128)(2,1)} %collective-permute-done.22.refs_4_), channel_id=1, source_target_pairs={{0,1},{1,0},{2,3},{3,2},{4,5},{5,4},{6,7},{7,6},{8,9},{9,8},{10,11... | collective-permute-start | bytes 9437192 | tf_op jit(solution)/shard_map/ppermute | solution.py:452
  192.9 14.5 %collective-permute-start.26 = (bf16[384,2048]{1,0:T(8,128)(2,1)S(1)}, bf16[384,2048]{1,0:T(8,128)(2,1)S(1)}, u32[]{:S(2)}, u32[]{:S(2)}) collective-permute-start(bf16[384,2048]{1,0:T(8,128)(2,1)S(1)} %collective-permute-done.20), channel_id=1, source_target_pairs={{4,6},{3,1},{12,14},{11,9},{20,22},{19,17},{28,30},{27,25}} | collective-permute-start | bytes 4718600 | tf_op jit(solution)/shard_map/ppermute | solution.py:457
  201.9 15.7 %collective-permute-start.25 = (bf16[384,2048]{1,0:T(8,128)(2,1)S(1)}, bf16[384,2048]{1,0:T(8,128)(2,1)S(1)}, u32[]{:S(2)}, u32[]{:S(2)}) collective-permute-start(bf16[384,2048]{1,0:T(8,128)(2,1)S(1)} %collective-permute-done.20), channel_id=1, source_target_pairs={{0,1},{1,0},{2,3},{3,2},{4,5},{5,4},{6,7},{7,6},{8,9},{9,8},{10,11... | collective-permute-start | bytes 4718600 | tf_op jit(solution)/shard_map/ppermute | solution.py:452
  203.8 30.9 %collective-permute-start.15 = (bf16[96,8192]{1,0:T(8,128)(2,1)}, bf16[96,8192]{1,0:T(8,128)(2,1)}, u32[]{:S(2)}, u32[]{:S(2)}) collective-permute-start(bf16[96,8192]{1,0:T(8,128)(2,1)} %get-tuple-element.97), channel_id=1, source_target_pairs={{0,1},{1,0},{2,3},{3,2},{4,5},{5,4},{6,7},{7,6},{8,9},{9,8},{10,11... | collective-permute-start | bytes 4718600 | tf_op jit(solution)/shard_map/ppermute | solution.py:452
  207.4 13.7 %collective-permute-start.27 = (bf16[384,2048]{1,0:T(8,128)(2,1)S(1)}, bf16[384,2048]{1,0:T(8,128)(2,1)S(1)}, u32[]{:S(2)}, u32[]{:S(2)}) collective-permute-start(bf16[384,2048]{1,0:T(8,128)(2,1)S(1)} %collective-permute-done.26), channel_id=1, source_target_pairs={{0,1},{1,0},{2,3},{3,2},{4,5},{5,4},{6,7},{7,6},{8,9},{9,8},{10,11... | collective-permute-start | bytes 4718600 | tf_op jit(solution)/shard_map/ppermute | solution.py:452
  214.7 20.0 %collective-permute-start.23 = (bf16[96,8192]{1,0:T(8,128)(2,1)}, bf16[96,8192]{1,0:T(8,128)(2,1)}, u32[]{:S(2)}, u32[]{:S(2)}) collective-permute-start(bf16[96,8192]{1,0:T(8,128)(2,1)} %add_convert_fusion.1), channel_id=1, source_target_pairs={{0,2},{2,4},{5,3},{7,5},{8,10},{10,12},{13,11},{15,13},{16,18},{18... | collective-permute-start | bytes 4718600 | tf_op jit(solution)/shard_map/ppermute | solution.py:457
  227.1 37.6 %collective-permute-start.31 = (bf16[384,4096]{1,0:T(8,128)(2,1)}, bf16[384,4096]{1,0:T(8,128)(2,1)}, u32[]{:S(2)}, u32[]{:S(2)}) collective-permute-start(bf16[384,4096]{1,0:T(8,128)(2,1)} %column_half.3), channel_id=1, source_target_pairs={{0,8},{1,17},{2,10},{3,19},{4,12},{5,21},{6,14},{7,23},{8,0},{9,25... | collective-permute-start | bytes 9437192 | tf_op jit(solution)/shard_map/ppermute | solution.py:561
  238.8 24.7 %collective-permute-start.28 = (bf16[96,8192]{1,0:T(8,128)(2,1)}, bf16[96,8192]{1,0:T(8,128)(2,1)}, u32[]{:S(2)}, u32[]{:S(2)}) collective-permute-start(bf16[96,8192]{1,0:T(8,128)(2,1)} %add_convert_fusion), channel_id=1, source_target_pairs={{0,2},{2,4},{4,6},{3,1},{5,3},{7,5},{8,10},{10,12},{12,14},{11,9},... | collective-permute-start | bytes 4718600 | tf_op jit(solution)/shard_map/ppermute | solution.py:457
  246.4 13.3 %copy-start.23 = (f32[384,1024]{1,0:T(8,128)S(1)}, f32[384,1024]{1,0:T(8,128)}, u32[]{:S(2)}) copy-start(f32[384,1024]{1,0:T(8,128)} %copy-done.22) | copy-start | bytes 4718596
  246.5 13.3 %copy-start.29 = (bf16[384,1024]{1,0:T(8,128)(2,1)S(1)}, bf16[384,1024]{1,0:T(8,128)(2,1)}, u32[]{:S(2)}) copy-start(bf16[384,1024]{1,0:T(8,128)(2,1)} %param.11) | copy-start | bytes 2359300
  261.3 6.9 %copy-start.37 = (s32[128]{0:T(128)S(1)}, s32[128]{0:T(128)}, u32[]{:S(2)}) copy-start(s32[128]{0:T(128)} %param.15) | copy-start | bytes 1540
  261.3 16.1 %copy-start.16 = (bf16[1024,384]{1,0:T(8,128)(2,1)S(1)}, bf16[1024,384]{1,0:T(8,128)(2,1)}, u32[]{:S(2)}) copy-start(bf16[1024,384]{1,0:T(8,128)(2,1)} %copy-done.15) | copy-start | bytes 2359300
  264.7 64.2 %collective-permute-start.33 = (bf16[384,4096]{1,0:T(8,128)(2,1)}, bf16[384,4096]{1,0:T(8,128)(2,1)}, u32[]{:S(2)}, u32[]{:S(2)}) collective-permute-start(bf16[384,4096]{1,0:T(8,128)(2,1)} %collective-permute-done.31.refs_4_), channel_id=1, source_target_pairs={{0,1},{1,0},{2,3},{3,2},{4,5},{5,4},{6,7},{7,6},{8,9},{9,8},{10,11... | collective-permute-start | bytes 9437192 | tf_op jit(solution)/shard_map/ppermute | solution.py:452
  266.0 26.9 %collective-permute-start.29 = (bf16[48,8192]{1,0:T(8,128)(2,1)S(1)}, bf16[48,8192]{1,0:T(8,128)(2,1)S(1)}, u32[]{:S(2)}, u32[]{:S(2)}) collective-permute-start(bf16[48,8192]{1,0:T(8,128)(2,1)S(1)} %fusion.5), channel_id=1, source_target_pairs={{0,1},{1,0},{2,3},{3,2},{4,5},{5,4},{6,7},{7,6},{8,9},{9,8},{10,11... | collective-permute-start | bytes 2359304 | tf_op jit(solution)/shard_map/ppermute | solution.py:452
  266.6 7.8 %collective-permute-start.35 = (bf16[2,256,384]{2,1,0:T(8,128)(2,1)S(1)}, bf16[2,256,384]{2,1,0:T(8,128)(2,1)S(1)}, u32[]{:S(2)}, u32[]{:S(2)}) collective-permute-start(bf16[2,256,384]{2,1,0:T(8,128)(2,1)S(1)} %copy-done.18), channel_id=1, source_target_pairs={{0,16},{1,9},{2,18},{3,11},{4,20},{5,13},{6,22},{7,15},{8,24},{9,1... | collective-permute-start | bytes 1179656 | tf_op jit(solution)/shard_map/ppermute | solution.py:561
  269.2 59.7 %collective-permute-start.32 = (bf16[2,256,384]{2,1,0:T(8,128)(2,1)S(1)}, bf16[2,256,384]{2,1,0:T(8,128)(2,1)}, u32[]{:S(2)}, u32[]{:S(2)}) collective-permute-start(bf16[2,256,384]{2,1,0:T(8,128)(2,1)S(1)} %get-tuple-element.76), channel_id=1, source_target_pairs={{0,16},{1,9},{2,18},{3,11},{4,20},{5,13},{6,22},{7,15},{8,24},{9,1... | collective-permute-start | bytes 1179656 | tf_op jit(solution)/shard_map/ppermute | solution.py:561
  274.4 44.3 %collective-permute-start.30 = (bf16[2,256,384]{2,1,0:T(8,128)(2,1)}, bf16[2,256,384]{2,1,0:T(8,128)(2,1)}, u32[]{:S(2)}, u32[]{:S(2)}) collective-permute-start(bf16[2,256,384]{2,1,0:T(8,128)(2,1)} %get-tuple-element.73), channel_id=1, source_target_pairs={{0,8},{1,17},{2,10},{3,19},{4,12},{5,21},{6,14},{7,23},{8,0},{9,25... | collective-permute-start | bytes 1179656 | tf_op jit(solution)/shard_map/ppermute | solution.py:561
  275.9 67.9 %collective-permute-start.34 = (bf16[256,4096]{1,0:T(8,128)(2,1)}, bf16[256,4096]{1,0:T(8,128)(2,1)}, u32[]{:S(2)}, u32[]{:S(2)}) collective-permute-start(bf16[256,4096]{1,0:T(8,128)(2,1)} %get-tuple-element.79), channel_id=1, source_target_pairs={{0,16},{1,9},{2,18},{3,11},{4,20},{5,13},{6,22},{7,15},{8,24},{9,1... | collective-permute-start | bytes 6291464 | tf_op jit(solution)/shard_map/ppermute | solution.py:561
  287.0 26.9 %all-to-all-start = ((bf16[8,48,1024]{2,1,0:T(8,128)(2,1)}), bf16[8,48,1024]{2,1,0:T(8,128)(2,1)S(1)}, u32[]{:S(2)}, u32[]{:S(2)}) async-start(bf16[8,48,1024]{2,1,0:T(8,128)(2,1)} %bitcast.16), calls=%async_computation | async-start | bytes 1572864 | tf_op jit(solution)/shard_map/all_to_all | solution.py:671
  293.0 50.9 %collective-permute-start.37 = (bf16[256,4096]{1,0:T(8,128)(2,1)}, bf16[256,4096]{1,0:T(8,128)(2,1)}, u32[]{:S(2)}, u32[]{:S(2)}) collective-permute-start(bf16[256,4096]{1,0:T(8,128)(2,1)} %get-tuple-element.83), channel_id=1, source_target_pairs={{0,8},{1,17},{2,10},{3,19},{4,12},{5,21},{6,14},{7,23},{8,0},{9,25... | collective-permute-start | bytes 6291464 | tf_op jit(solution)/shard_map/ppermute | solution.py:561
  295.2 23.5 %copy-start.14 = (bf16[1024,384]{1,0:T(8,128)(2,1)S(1)}, bf16[1024,384]{1,0:T(8,128)(2,1)}, u32[]{:S(2)}) copy-start(bf16[1024,384]{1,0:T(8,128)(2,1)} %copy-done.13) | copy-start | bytes 2359300
  328.4 92.6 %collective-permute-start.38 = (bf16[256,4096]{1,0:T(8,128)(2,1)}, bf16[256,4096]{1,0:T(8,128)(2,1)}, u32[]{:S(2)}, u32[]{:S(2)}) collective-permute-start(bf16[256,4096]{1,0:T(8,128)(2,1)} %get-tuple-element.88), channel_id=1, source_target_pairs={{0,16},{1,9},{2,18},{3,11},{4,20},{5,13},{6,22},{7,15},{8,24},{9,1... | collective-permute-start | bytes 6291464 | tf_op jit(solution)/shard_map/ppermute | solution.py:561
  328.9 13.9 %copy-start.36 = (f32[2,256]{1,0:T(2,128)S(1)}, f32[2,256]{1,0:T(2,128)}, u32[]{:S(2)}) copy-start(f32[2,256]{1,0:T(2,128)} %param.14) | copy-start | bytes 6148
  328.9 14.0 %copy-start.33 = (s32[4,1536,4]{1,2,0:T(4,128)S(1)}, s32[4,1536,4]{1,2,0:T(4,128)}, u32[]{:S(2)}) copy-start(s32[4,1536,4]{1,2,0:T(4,128)} %param.16) | copy-start | bytes 294916
  328.9 14.0 %copy-start.34 = (s32[4,1536]{1,0:T(4,128)S(1)}, s32[4,1536]{1,0:T(4,128)}, u32[]{:S(2)}) copy-start(s32[4,1536]{1,0:T(4,128)} %param.17) | copy-start | bytes 73732
  338.7 82.3 %collective-permute-start.39 = (bf16[256,4096]{1,0:T(8,128)(2,1)}, bf16[256,4096]{1,0:T(8,128)(2,1)}, u32[]{:S(2)}, u32[]{:S(2)}) collective-permute-start(bf16[256,4096]{1,0:T(8,128)(2,1)} %get-tuple-element.89), channel_id=1, source_target_pairs={{0,8},{1,17},{2,10},{3,19},{4,12},{5,21},{6,14},{7,23},{8,0},{9,25... | collective-permute-start | bytes 6291464 | tf_op jit(solution)/shard_map/ppermute | solution.py:561
  339.2 46.1 %all-to-all-start.1 = ((bf16[32,2,48,128]{3,2,1,0:T(8,128)(2,1)}), bf16[32,2,48,128]{3,2,1,0:T(8,128)(2,1)S(1)}, u32[]{:S(2)}, u32[]{:S(2)}) async-start(bf16[32,2,48,128]{3,2,1,0:T(8,128)(2,1)} %to_slots.1), calls=%async_computation.1 | async-start | bytes 1572864 | tf_op jit(solution)/shard_map/all_to_all | solution.py:686
  386.2 34.8 %copy-start.10 = (bf16[256,4096]{1,0:T(8,128)(2,1)S(1)}, bf16[256,4096]{1,0:T(8,128)(2,1)}, u32[]{:S(2)}) copy-start(bf16[256,4096]{1,0:T(8,128)(2,1)} %copy-done.9) | copy-start | bytes 6291460
  386.2 34.8 %copy-start.12 = (bf16[256,4096]{1,0:T(8,128)(2,1)S(1)}, bf16[256,4096]{1,0:T(8,128)(2,1)}, u32[]{:S(2)}) copy-start(bf16[256,4096]{1,0:T(8,128)(2,1)} %copy-done.11) | copy-start | bytes 6291460
  (16 other events, 42.0 us)
where the time goes:
time: 432 us; the launch traced here: 430 us
  Pallas kernels  154 us (36%)
  waiting for transfers between devices  109 us (25%)
  starting transfers between devices  87.4 us (20%)
  other arithmetic  63.7 us (15%)
  local copies, waits for them, and re-layouts  15.6 us (4%)
    ppermute x12, starting transfers between devices, hop(): return lax.ppermute(value, 'mp', pairs)  52.2 us
    pallas_call x1, Pallas kernels, embed_update(): pl.pallas_call(kern, out_shape=(jax.ShapeDtypeStruct(tables_t.shape, jnp....  34.8 us
    pallas_call x4, Pallas kernels, half_grad(): pl.pallas_call(functools.partial(grad_kernel, parts), out_shape=[jax.Shap...  33.3 us
    ppermute x10, waiting for transfers between devices, cross(): return lax.ppermute(value, ('dp', 'mp'), crossing(low_core, high_core))  32.3 us
    all_to_all x1, waiting for transfers between devices, body(): lax.all_to_all(slotted, ('dp', 'mp'), split_axis=0, concat_axis=0, tiled=...  31.2 us
    pallas_call x2, Pallas kernels, forward_product(): pl.pallas_call(forward_kernel, out_shape=jax.ShapeDtypeStruct((rows, widt...  26.4 us
    dynamic_update_slice x12, other arithmetic, gather_and_reduce(): lax.dynamic_update_slice_in_dim(wide, jnp.where(here, piece, chip), jnp.w...  23 us
    ppermute x12, waiting for transfers between devices, hop(): return lax.ppermute(value, 'mp', pairs)  21.8 us
  transfers between devices with their start and end apart: 42, of which 13 were waited for; matrix products, arithmetic and copies ran while one was open for 13% of the time, Pallas kernels for 32%

commit v1 on v0

--- a/solution.py
+++ b/solution.py
@@ -383,8 +383,9 @@
         value = joined[:, pl.ds(start, lanes)]
         return value, first - start
 
-    def one(device, carry):
-        for p in range(pairs):
+    def one(turn_idx, carry):
+        for u, p in ((u, p) for u in range(2) for p in range(pairs)):
+            device = turn_idx * 2 + u
             slot = device * per_device + 2 * p
             low, low_at = look(slot)
             high, high_at = look(slot + min(1, per_device - 1 - 2 * p))
@@ -393,7 +394,7 @@
             out_ref[device, p] = jnp.where(lane < embed, low, high).astype(out_ref.dtype)
         return carry
 
-    lax.fori_loop(0, devices, one, 0)
+    lax.fori_loop(0, devices // 2, one, 0)
 
 
 def to_slots(table_of, summed, late, embed, devices):

time: 432 us -> 431 us (level)
  no operation moved by 1% of the time
where the time goes in v1:
time: 431 us; the launch traced here: 429 us
  Pallas kernels  152 us (35%)
  waiting for transfers between devices  109 us (25%)
  starting transfers between devices  87.4 us (20%)
  other arithmetic  63.7 us (15%)
  local copies, waits for them, and re-layouts  15.6 us (4%)
    ppermute x12, starting transfers between devices, hop(): return lax.ppermute(value, 'mp', pairs)  52.2 us
    pallas_call x1, Pallas kernels, embed_update(): pl.pallas_call(kern, out_shape=(jax.ShapeDtypeStruct(tables_t.shape, jnp....  34.8 us
    pallas_call x4, Pallas kernels, half_grad(): pl.pallas_call(functools.partial(grad_kernel, parts), out_shape=[jax.Shap...  33.3 us
    ppermute x10, waiting for transfers between devices, cross(): return lax.ppermute(value, ('dp', 'mp'), crossing(low_core, high_core))  32.3 us
    all_to_all x1, waiting for transfers between devices, body(): lax.all_to_all(slotted, ('dp', 'mp'), split_axis=0, concat_axis=0, tiled=...  31.2 us
    pallas_call x2, Pallas kernels, forward_product(): pl.pallas_call(forward_kernel, out_shape=jax.ShapeDtypeStruct((rows, widt...  26.4 us
    dynamic_update_slice x12, other arithmetic, gather_and_reduce(): lax.dynamic_update_slice_in_dim(wide, jnp.where(here, piece, chip), jnp.w...  23 us
    ppermute x12, waiting for transfers between devices, hop(): return lax.ppermute(value, 'mp', pairs)  21.8 us
  transfers between devices with their start and end apart: 42, of which 13 were waited for; matrix products, arithmetic and copies ran while one was open for 13% of the time, Pallas kernels for 32%

profile of v1, /device:TPU:0, one launch (start us, length us, event | category | flops | bytes accessed | tf_op | source)
XLA Modules:
  0.0 429.1 jit_solution(4278188335425400670)
XLA Ops:
  1.3 2.0 collective-permute-done
  3.3 1.9 constant_dynamic-update-slice_fusion.1
  5.5 7.0 %column_blocks.2 = bf16[2,384,2048]{2,1,0:T(8,128)(2,1)S(1)} custom-call(s32[2]{0:T(128)S(1)} %get-tuple-element.114.index_ref, bf16[384,1024]{1,0:T(8,128)(2,1)S(1)} %fusion.2.value_ref, bf16[2,1024,8192]{2,1,0:T(8,128)(2,1)} %weight_ref.7), custom_call_target="tpu_custom_call" | custom-call | flops 3221225472 | bytes 11534336 | tf_op jit(solution)/shard_map/column_blocks/pallas_call | solution.py:208
  13.2 5.8 %collective-permute-start.6 = (bf16[384,2048]{1,0:T(8,128)(2,1)S(1)}, bf16[384,2048]{1,0:T(8,128)(2,1)}, u32[]{:S(2)}, u32[]{:S(2)}) collective-permute-start(bf16[384,2048]{1,0:T(8,128)(2,1)S(1)} %get-tuple-element.99), channel_id=1, source_target_pairs={{0,2},{2,4},{4,6},{3,1},{5,3},{7,5},{8,10},{10,12},{12,14},{11,9},... | collective-permute-start | bytes 4718600 | tf_op jit(solution)/shard_map/ppermute | solution.py:458
  18.9 7.0 %column_blocks.3 = bf16[2,384,2048]{2,1,0:T(8,128)(2,1)S(1)} custom-call(s32[2]{0:T(128)S(1)} %get-tuple-element.50.index_ref, bf16[384,1024]{1,0:T(8,128)(2,1)S(1)} %fusion.2.value_ref, bf16[2,1024,8192]{2,1,0:T(8,128)(2,1)} %weight_ref.7), custom_call_target="tpu_custom_call" | custom-call | flops 3221225472 | bytes 11534336 | tf_op jit(solution)/shard_map/column_blocks/pallas_call | solution.py:208
  26.0 2.7 add_convert_fusion.5
  28.6 7.0 %collective-permute-done.6 = bf16[384,2048]{1,0:T(8,128)(2,1)} collective-permute-done((bf16[384,2048]{1,0:T(8,128)(2,1)S(1)}, bf16[384,2048]{1,0:T(8,128)(2,1)}, u32[]{:S(2)}, u32[]{:S(2)}) %collective-permute-start.6) | collective-permute-done | bytes 1572896 | tf_op jit(solution)/shard_map/ppermute | solution.py:458
  35.7 2.0 collective-permute-start.8
  37.7 8.5 %collective-permute-start.4 = (bf16[384,2048]{1,0:T(8,128)(2,1)}, bf16[384,2048]{1,0:T(8,128)(2,1)}, u32[]{:S(2)}, u32[]{:S(2)}) collective-permute-start(bf16[384,2048]{1,0:T(8,128)(2,1)} %get-tuple-element.100), channel_id=1, source_target_pairs={{0,2},{7,5},{8,10},{15,13},{16,18},{23,21},{24,26},{31,29}} | collective-permute-start | bytes 4718600 | tf_op jit(solution)/shard_map/ppermute | solution.py:458
  46.2 2.0 fusion.15
  53.4 3.4 select_dynamic-update-slice_fusion.11
  56.8 6.5 %collective-permute-done.4 = bf16[384,2048]{1,0:T(8,128)(2,1)} collective-permute-done((bf16[384,2048]{1,0:T(8,128)(2,1)}, bf16[384,2048]{1,0:T(8,128)(2,1)}, u32[]{:S(2)}, u32[]{:S(2)}) %collective-permute-start.4) | collective-permute-done | bytes 1572896 | tf_op jit(solution)/shard_map/ppermute | solution.py:458
  63.2 3.9 add_convert_fusion.4
  67.1 5.5 %collective-permute-start.5 = (bf16[384,2048]{1,0:T(8,128)(2,1)}, bf16[384,2048]{1,0:T(8,128)(2,1)}, u32[]{:S(2)}, u32[]{:S(2)}) collective-permute-start(bf16[384,2048]{1,0:T(8,128)(2,1)} %add_convert_fusion.4), channel_id=1, source_target_pairs={{0,2},{2,4},{5,3},{7,5},{8,10},{10,12},{13,11},{15,13},{16,18},{18... | collective-permute-start | bytes 4718600 | tf_op jit(solution)/shard_map/ppermute | solution.py:458
  72.6 1.8 select_dynamic-update-slice_fusion.10
  74.4 4.6 %collective-permute-start.11 = (bf16[384,2048]{1,0:T(8,128)(2,1)S(1)}, bf16[384,2048]{1,0:T(8,128)(2,1)S(1)}, u32[]{:S(2)}, u32[]{:S(2)}) collective-permute-start(bf16[384,2048]{1,0:T(8,128)(2,1)S(1)} %collective-permute-done.10), channel_id=1, source_target_pairs={{0,1},{1,0},{2,3},{3,2},{4,5},{5,4},{6,7},{7,6},{8,9},{9,8},{10,11... | collective-permute-start | bytes 4718600 | tf_op jit(solution)/shard_map/ppermute | solution.py:453
  79.0 1.8 select_dynamic-update-slice_fusion.9
  80.8 1.8 select_dynamic-update-slice_fusion.8
  82.5 1.8 select_dynamic-update-slice_fusion.7
  84.3 1.8 select_dynamic-update-slice_fusion.6.value_ref.wide_ref.refs_3_
  86.0 4.2 column_half.2
  90.3 4.2 add_convert_fusion.3
  94.5 6.5 %collective-permute-start.12 = (bf16[384,2048]{1,0:T(8,128)(2,1)}, bf16[384,2048]{1,0:T(8,128)(2,1)}, u32[]{:S(2)}, u32[]{:S(2)}) collective-permute-start(bf16[384,2048]{1,0:T(8,128)(2,1)} %add_convert_fusion.3), channel_id=1, source_target_pairs={{0,2},{2,4},{4,6},{3,1},{5,3},{7,5},{8,10},{10,12},{12,14},{11,9},... | collective-permute-start | bytes 4718600 | tf_op jit(solution)/shard_map/ppermute | solution.py:458
  101.0 13.2 %forward_product.2 = f32[384,1024]{1,0:T(8,128)S(1)} custom-call(bf16[384,8192]{1,0:T(8,128)(2,1)} %select_dynamic-update-slice_fusion.6.value_ref.wide_ref.refs_3_, bf16[2,1024,8192]{2,1,0:T(8,128)(2,1)} %weight_ref.7, f32[1,1024]{1,0:T(1,128)S(1)} %get-tuple-element.108.bias_ref), custom_call_target="tpu_custom_call" | custom-call | flops 6442450944 | bytes 23068672 | tf_op jit(solution)/shard_map/forward_product/pallas_call | solution.py:284
  114.6 2.2 collective-permute-done.13
  116.8 2.4 constant_dynamic-update-slice_fusion
  119.2 2.4 fusion.7
  121.9 5.5 %collective-permute-start.19 = (bf16[384,2048]{1,0:T(8,128)(2,1)}, bf16[384,2048]{1,0:T(8,128)(2,1)}, u32[]{:S(2)}, u32[]{:S(2)}) collective-permute-start(bf16[384,2048]{1,0:T(8,128)(2,1)} %get-tuple-element.95), channel_id=1, source_target_pairs={{0,2},{2,4},{4,6},{3,1},{5,3},{7,5},{8,10},{10,12},{12,14},{11,9},... | collective-permute-start | bytes 4718600 | tf_op jit(solution)/shard_map/ppermute | solution.py:458
  127.4 2.2 convert_add_fusion.1
  131.0 12.4 %row_blocks_product.1 = bf16[4,96,8192]{2,1,0:T(8,128)(2,1)S(1)} custom-call(s32[4]{0:T(128)S(1)} %pad_add_fusion.index_ref, bf16[384,1024]{1,0:T(8,128)(2,1)S(1)} %fusion.4.refs_0_.refs_1_.refs_2_.refs_3_.value_ref, bf16[384,1024]{1,0:T(8,128)(2,1)S(1)} %fusion.4.refs_0_.refs_1_.refs_2_.refs_3_.value_ref, ...), custom_call_target="tpu_custom_call" | custom-call | flops 6442450944 | bytes 23068672 | tf_op jit(solution)/shard_map/row_blocks_product/pallas_call | solution.py:247
  143.4 2.4 fusion.14
  145.8 1.8 copy-done
  151.3 4.5 %add_convert_fusion.2 = (bf16[96,8192]{1,0:T(8,128)(2,1)S(1)}, bf16[96,8192]{1,0:T(8,128)(2,1)}) fusion(bf16[96,8192]{1,0:T(8,128)(2,1)} %collective-permute-done.17, bf16[4,96,8192]{2,1,0:T(8,128)(2,1)} %copy-done, pred[]{:T(512)S(6)} %eq.24), kind=kLoop, calls=%fused_computation.3 | loop fusion | flops 3932160 | bytes 7864321 | tf_op jit(solution)/shard_map/convert_element_type | solution.py:533
  155.8 5.6 %collective-permute-start.18 = (bf16[96,8192]{1,0:T(8,128)(2,1)S(1)}, bf16[96,8192]{1,0:T(8,128)(2,1)S(1)}, u32[]{:S(2)}, u32[]{:S(2)}) collective-permute-start(bf16[96,8192]{1,0:T(8,128)(2,1)S(1)} %get-tuple-element.96), channel_id=1, source_target_pairs={{0,2},{7,5},{8,10},{15,13},{16,18},{23,21},{24,26},{31,29}} | collective-permute-start | bytes 4718600 | tf_op jit(solution)/shard_map/ppermute | solution.py:458
  162.4 22.7 %collective-permute-done.22.refs_4_ = bf16[384,4096]{1,0:T(8,128)(2,1)} collective-permute-done((bf16[384,4096]{1,0:T(8,128)(2,1)}, bf16[384,4096]{1,0:T(8,128)(2,1)}, u32[]{:S(2)}, u32[]{:S(2)}) %collective-permute-start.22) | collective-permute-done | bytes 3145760 | tf_op jit(solution)/shard_map/ppermute | solution.py:562
  186.6 1.8 select_dynamic-update-slice_fusion.5
  189.3 3.6 collective-permute-done.21.refs_2_
  193.7 8.2 %half_grad.4 = (bf16[256,4096]{1,0:T(8,128)(2,1)S(1)}, bf16[256,4096]{1,0:T(8,128)(2,1)}) custom-call(s32[3]{0:T(128)S(1)} %pad_add_fusion.4.index_ref, bf16[1024,384]{1,0:T(8,128)(2,1)S(1)} %get-tuple-element.63.refs_0_.refs_1_, bf16[1024,384]{1,0:T(8,128)(2,1)S(1)} %get-tuple-element.63.refs_0_.refs_1_, ...), custom_call_target="tpu_custom_call" | custom-call | flops 3221225472 | bytes 10485760 | tf_op jit(solution)/shard_map/half_grad/pallas_call | solution.py:149
  201.9 1.8 select_dynamic-update-slice_fusion.4
  204.3 3.1 add_convert_fusion.1
  207.4 5.4 %collective-permute-start.27 = (bf16[384,2048]{1,0:T(8,128)(2,1)S(1)}, bf16[384,2048]{1,0:T(8,128)(2,1)S(1)}, u32[]{:S(2)}, u32[]{:S(2)}) collective-permute-start(bf16[384,2048]{1,0:T(8,128)(2,1)S(1)} %collective-permute-done.26), channel_id=1, source_target_pairs={{0,1},{1,0},{2,3},{3,2},{4,5},{5,4},{6,7},{7,6},{8,9},{9,8},{10,11... | collective-permute-start | bytes 4718600 | tf_op jit(solution)/shard_map/ppermute | solution.py:453
  212.9 1.8 select_dynamic-update-slice_fusion.3
  214.7 2.9 collective-permute-start.23
  217.6 1.7 select_dynamic-update-slice_fusion.2
  219.3 1.8 select_dynamic-update-slice_fusion.1
  221.1 1.8 select_dynamic-update-slice_fusion.value_ref.wide_ref.refs_3_
  222.9 4.2 column_half.3
  228.6 6.0 %collective-permute-done.23 = bf16[96,8192]{1,0:T(8,128)(2,1)} collective-permute-done((bf16[96,8192]{1,0:T(8,128)(2,1)}, bf16[96,8192]{1,0:T(8,128)(2,1)}, u32[]{:S(2)}, u32[]{:S(2)}) %collective-permute-start.23) | collective-permute-done | bytes 1572896 | tf_op jit(solution)/shard_map/ppermute | solution.py:458
  234.6 4.2 add_convert_fusion
  238.8 7.6 %collective-permute-start.28 = (bf16[96,8192]{1,0:T(8,128)(2,1)}, bf16[96,8192]{1,0:T(8,128)(2,1)}, u32[]{:S(2)}, u32[]{:S(2)}) collective-permute-start(bf16[96,8192]{1,0:T(8,128)(2,1)} %add_convert_fusion), channel_id=1, source_target_pairs={{0,2},{2,4},{4,6},{3,1},{5,3},{7,5},{8,10},{10,12},{12,14},{11,9},... | collective-permute-start | bytes 4718600 | tf_op jit(solution)/shard_map/ppermute | solution.py:458
  246.5 13.3 %forward_product.3 = f32[384,1024]{1,0:T(8,128)S(1)} custom-call(bf16[384,8192]{1,0:T(8,128)(2,1)} %select_dynamic-update-slice_fusion.value_ref.wide_ref.refs_3_, bf16[2,1024,8192]{2,1,0:T(8,128)(2,1)} %weight_ref.7, f32[1,1024]{1,0:T(1,128)S(1)} %get-tuple-element.107.bias_ref), custom_call_target="tpu_custom_call" | custom-call | flops 6442450944 | bytes 23068672 | tf_op jit(solution)/shard_map/forward_product/pallas_call | solution.py:284
  261.3 2.2 collective-permute-done.28
  269.7 4.7 %collective-permute-done.35.refs_2_ = bf16[2,256,384]{2,1,0:T(8,128)(2,1)S(1)} collective-permute-done((bf16[2,256,384]{2,1,0:T(8,128)(2,1)S(1)}, bf16[2,256,384]{2,1,0:T(8,128)(2,1)S(1)}, u32[]{:S(2)}, u32[]{:S(2)}) %collective-permute-start.35) | collective-permute-done | bytes 393248 | tf_op jit(solution)/shard_map/ppermute | solution.py:562
  277.4 8.3 %half_grad.7 = (bf16[256,4096]{1,0:T(8,128)(2,1)S(1)}, bf16[256,4096]{1,0:T(8,128)(2,1)}) custom-call(s32[3]{0:T(128)S(1)} %pad_add_fusion.5.index_ref, bf16[1024,384]{1,0:T(8,128)(2,1)S(1)} %copy-done.16, bf16[1024,384]{1,0:T(8,128)(2,1)S(1)} %copy-done.16, bf16[2,256,384]{2,1,0:T(8,128)(2,1)S(1)} %collective-permute-done.35.refs_2_, ...), custom_call_target="tpu_custom_call" | custom-call | flops 3221225472 | bytes 10485760 | tf_op jit(solution)/shard_map/half_grad/pallas_call | solution.py:149
  287.0 5.9 %all-to-all-start = ((bf16[8,48,1024]{2,1,0:T(8,128)(2,1)}), bf16[8,48,1024]{2,1,0:T(8,128)(2,1)S(1)}, u32[]{:S(2)}, u32[]{:S(2)}) async-start(bf16[8,48,1024]{2,1,0:T(8,128)(2,1)} %bitcast.16), calls=%async_computation | async-start | bytes 1572864 | tf_op jit(solution)/shard_map/all_to_all | solution.py:672
  295.2 18.7 %all-to-all-done.late_ref = bf16[8,48,1024]{2,1,0:T(8,128)(2,1)S(1)} async-done(((bf16[8,48,1024]{2,1,0:T(8,128)(2,1)}), bf16[8,48,1024]{2,1,0:T(8,128)(2,1)S(1)}, u32[]{:S(2)}, u32[]{:S(2)}) %all-to-all-start) | async-done | bytes 786464 | tf_op jit(solution)/shard_map/all_to_all | solution.py:672
  313.9 3.6 to_slots.1
  317.5 8.4 %half_grad.5 = (bf16[256,4096]{1,0:T(8,128)(2,1)S(1)}, bf16[256,4096]{1,0:T(8,128)(2,1)}) custom-call(s32[3]{0:T(128)S(1)} %pad_add_fusion.4.index_ref, bf16[1024,384]{1,0:T(8,128)(2,1)S(1)} %copy-done.14, bf16[1024,384]{1,0:T(8,128)(2,1)S(1)} %copy-done.14, bf16[2,256,384]{2,1,0:T(8,128)(2,1)} %collective-permute-done.30.refs_2_, ...), custom_call_target="tpu_custom_call" | custom-call | flops 3221225472 | bytes 10485760 | tf_op jit(solution)/shard_map/half_grad/pallas_call | solution.py:149
  327.7 8.4 %half_grad.6 = (bf16[256,4096]{1,0:T(8,128)(2,1)S(1)}, bf16[256,4096]{1,0:T(8,128)(2,1)}) custom-call(s32[3]{0:T(128)S(1)} %pad_add_fusion.5.index_ref, bf16[1024,384]{1,0:T(8,128)(2,1)S(1)} %copy-done.14, bf16[1024,384]{1,0:T(8,128)(2,1)S(1)} %copy-done.14, bf16[2,256,384]{2,1,0:T(8,128)(2,1)} %collective-permute-done.32.refs_2_, ...), custom_call_target="tpu_custom_call" | custom-call | flops 3221225472 | bytes 10485760 | tf_op jit(solution)/shard_map/half_grad/pallas_call | solution.py:149
  338.0 3.6 all-to-all-start.1
  344.2 8.5 %weight_update.2 = (f32[2,256,8192]{2,1,0:T(8,128)}, f32[256,1]{1,0:T(8,128)S(1)}) custom-call(s32[1]{0:T(128)} %bitcast.index_ref.side_ref, f32[256,1]{1,0:T(8,128)S(1)} %copy.15.accum_ref, bf16[256,4096]{1,0:T(8,128)(2,1)S(1)} %copy-done.6, bf16[256,4096]{1,0:T(8,128)(2,1)} %collective-permute-done.34.refs_1_, bf16[256,4096]{1,0:T(8,128)(2,1)S(1)} %copy-done.8, ...), custom_call_target="tpu_custom_call" | custom-call | flops 8388608 | bytes 16777216 | tf_op jit(solution)/shard_map/weight_update/pallas_call | solution.py:346
  352.9 31.2 %all-to-all-done.1.g_ref = bf16[32,2,48,128]{3,2,1,0:T(8,128)(2,1)S(1)} async-done(((bf16[32,2,48,128]{3,2,1,0:T(8,128)(2,1)}), bf16[32,2,48,128]{3,2,1,0:T(8,128)(2,1)S(1)}, u32[]{:S(2)}, u32[]{:S(2)}) %all-to-all-start.1) | async-done | bytes 786464 | tf_op jit(solution)/shard_map/all_to_all | solution.py:687
  385.0 34.8 %embed_update.1 = (f32[4,64,8192]{2,1,0:T(8,128)}, f32[4,8192]{1,0:T(4,128)}) custom-call(s32[24576]{0:T(1024)} %reshape.35.ids_ref, bf16[32,2,48,128]{3,2,1,0:T(8,128)(2,1)} %copy-done.32, f32[4,64,8192]{2,1,0:T(8,128)} %bitcast.49, f32[4,8192]{1,0:T(4,128)} %acc_in_ref.1), custom_call_target="tpu_custom_call" | custom-call | flops 100000000 | bytes 150000000 | tf_op jit(solution)/shard_map/embed_update/pallas_call | solution.py:64
  419.9 8.5 %weight_update.3 = (f32[2,256,8192]{2,1,0:T(8,128)}, f32[256,1]{1,0:T(8,128)S(1)}) custom-call(s32[1]{0:T(128)} %bitcast.index_ref.side_ref, f32[256,1]{1,0:T(8,128)S(1)} %copy.16.accum_ref, bf16[256,4096]{1,0:T(8,128)(2,1)S(1)} %copy-done.10, bf16[256,4096]{1,0:T(8,128)(2,1)} %collective-permute-done.38.refs_1_, ...), custom_call_target="tpu_custom_call", output_to_operand_aliasing={{0}: (6, {})} | custom-call | flops 8388608 | bytes 16777216 | tf_op jit(solution)/shard_map/weight_update/pallas_call | solution.py:346
  (166 shorter events, 40.9 us)
Async XLA Ops:
  0.6 2.7 collective-permute-start
  5.2 7.9 %copy-start.19 = (bf16[384,2048]{1,0:T(8,128)(2,1)}, bf16[384,2048]{1,0:T(8,128)(2,1)S(1)}, u32[]{:S(2)}) copy-start(bf16[384,2048]{1,0:T(8,128)(2,1)S(1)} %get-tuple-element.99) | copy-start | bytes 4718596
  5.5 13.4 %copy-start.3 = (bf16[384,1024]{1,0:T(8,128)(2,1)}, bf16[384,1024]{1,0:T(8,128)(2,1)S(1)}, u32[]{:S(2)}) copy-start(bf16[384,1024]{1,0:T(8,128)(2,1)S(1)} %fusion.2.value_ref) | copy-start | bytes 2359300
  12.7 13.2 %collective-permute-start.3 = (bf16[384,2048]{1,0:T(8,128)(2,1)S(1)}, bf16[384,2048]{1,0:T(8,128)(2,1)S(1)}, u32[]{:S(2)}, u32[]{:S(2)}) collective-permute-start(bf16[384,2048]{1,0:T(8,128)(2,1)S(1)} %select_bitcast_fusion.3), channel_id=1, source_target_pairs={{0,1},{1,0},{2,3},{3,2},{4,5},{5,4},{6,7},{7,6},{8,9},{9,8},{10,11... | collective-permute-start | bytes 4718600 | tf_op jit(solution)/shard_map/ppermute | solution.py:453
  13.2 22.5 %collective-permute-start.6 = (bf16[384,2048]{1,0:T(8,128)(2,1)S(1)}, bf16[384,2048]{1,0:T(8,128)(2,1)}, u32[]{:S(2)}, u32[]{:S(2)}) collective-permute-start(bf16[384,2048]{1,0:T(8,128)(2,1)S(1)} %get-tuple-element.99), channel_id=1, source_target_pairs={{0,2},{2,4},{4,6},{3,1},{5,3},{7,5},{8,10},{10,12},{12,14},{11,9},... | collective-permute-start | bytes 4718600 | tf_op jit(solution)/shard_map/ppermute | solution.py:458
  25.9 20.3 %copy-start.1 = (bf16[2,384,2048]{2,1,0:T(8,128)(2,1)}, bf16[2,384,2048]{2,1,0:T(8,128)(2,1)S(1)}, u32[]{:S(2)}) copy-start(bf16[2,384,2048]{2,1,0:T(8,128)(2,1)S(1)} %column_blocks.3) | copy-start | bytes 9437188
  35.7 13.2 %copy-start.35 = (f32[2,1024]{1,0:T(2,128)S(1)}, f32[2,1024]{1,0:T(2,128)}, u32[]{:S(2)}) copy-start(f32[2,1024]{1,0:T(2,128)} %param.13) | copy-start | bytes 24580
  35.7 16.9 %collective-permute-start.8 = (bf16[384,2048]{1,0:T(8,128)(2,1)}, bf16[384,2048]{1,0:T(8,128)(2,1)}, u32[]{:S(2)}, u32[]{:S(2)}) collective-permute-start(bf16[384,2048]{1,0:T(8,128)(2,1)} %collective-permute-done.6), channel_id=1, source_target_pairs={{2,4},{4,6},{3,1},{5,3},{10,12},{12,14},{11,9},{13,11},{18,20},{20... | collective-permute-start | bytes 4718600 | tf_op jit(solution)/shard_map/ppermute | solution.py:458
  37.7 25.5 %collective-permute-start.4 = (bf16[384,2048]{1,0:T(8,128)(2,1)}, bf16[384,2048]{1,0:T(8,128)(2,1)}, u32[]{:S(2)}, u32[]{:S(2)}) collective-permute-start(bf16[384,2048]{1,0:T(8,128)(2,1)} %get-tuple-element.100), channel_id=1, source_target_pairs={{0,2},{7,5},{8,10},{15,13},{16,18},{23,21},{24,26},{31,29}} | collective-permute-start | bytes 4718600 | tf_op jit(solution)/shard_map/ppermute | solution.py:458
  48.2 15.0 %collective-permute-start.2 = (bf16[384,2048]{1,0:T(8,128)(2,1)}, bf16[384,2048]{1,0:T(8,128)(2,1)}, u32[]{:S(2)}, u32[]{:S(2)}) collective-permute-start(bf16[384,2048]{1,0:T(8,128)(2,1)} %get-tuple-element.106), channel_id=1, source_target_pairs={{0,1},{1,0},{2,3},{3,2},{4,5},{5,4},{6,7},{7,6},{8,9},{9,8},{10,11... | collective-permute-start | bytes 4718600 | tf_op jit(solution)/shard_map/ppermute | solution.py:453
  48.2 24.4 %collective-permute-start.7 = (bf16[384,2048]{1,0:T(8,128)(2,1)}, bf16[384,2048]{1,0:T(8,128)(2,1)S(1)}, u32[]{:S(2)}, u32[]{:S(2)}) collective-permute-start(bf16[384,2048]{1,0:T(8,128)(2,1)} %collective-permute-done.6), channel_id=1, source_target_pairs={{0,1},{1,0},{2,3},{3,2},{4,5},{5,4},{6,7},{7,6},{8,9},{9,8},{10,11... | collective-permute-start | bytes 4718600 | tf_op jit(solution)/shard_map/ppermute | solution.py:453
  52.6 37.7 %collective-permute-start.1 = (bf16[384,2048]{1,0:T(8,128)(2,1)}, bf16[384,2048]{1,0:T(8,128)(2,1)}, u32[]{:S(2)}, u32[]{:S(2)}) collective-permute-start(bf16[384,2048]{1,0:T(8,128)(2,1)} %get-tuple-element.101), channel_id=1, source_target_pairs={{0,1},{1,0},{2,3},{3,2},{4,5},{5,4},{6,7},{7,6},{8,9},{9,8},{10,11... | collective-permute-start | bytes 4718600 | tf_op jit(solution)/shard_map/ppermute | solution.py:453
  52.6 21.8 %collective-permute-start.10 = (bf16[384,2048]{1,0:T(8,128)(2,1)}, bf16[384,2048]{1,0:T(8,128)(2,1)S(1)}, u32[]{:S(2)}, u32[]{:S(2)}) collective-permute-start(bf16[384,2048]{1,0:T(8,128)(2,1)} %collective-permute-done.8), channel_id=1, source_target_pairs={{4,6},{3,1},{12,14},{11,9},{20,22},{19,17},{28,30},{27,25}} | collective-permute-start | bytes 4718600 | tf_op jit(solution)/shard_map/ppermute | solution.py:458
  53.3 9.9 %copy-start.2 = (bf16[2,384,2048]{2,1,0:T(8,128)(2,1)S(1)}, bf16[2,384,2048]{2,1,0:T(8,128)(2,1)}, u32[]{:S(2)}) copy-start(bf16[2,384,2048]{2,1,0:T(8,128)(2,1)} %copy-done.1) | copy-start | bytes 9437188
  56.8 15.9 %copy-start.20 = (bf16[384,2048]{1,0:T(8,128)(2,1)S(1)}, bf16[384,2048]{1,0:T(8,128)(2,1)}, u32[]{:S(2)}) copy-start(bf16[384,2048]{1,0:T(8,128)(2,1)} %copy-done.19) | copy-start | bytes 4718596
  63.2 17.5 %collective-permute-start.9 = (bf16[384,2048]{1,0:T(8,128)(2,1)}, bf16[384,2048]{1,0:T(8,128)(2,1)S(1)}, u32[]{:S(2)}, u32[]{:S(2)}) collective-permute-start(bf16[384,2048]{1,0:T(8,128)(2,1)} %collective-permute-done.8), channel_id=1, source_target_pairs={{0,1},{1,0},{2,3},{3,2},{4,5},{5,4},{6,7},{7,6},{8,9},{9,8},{10,11... | collective-permute-start | bytes 4718600 | tf_op jit(solution)/shard_map/ppermute | solution.py:453
  67.1 23.1 %collective-permute-start.5 = (bf16[384,2048]{1,0:T(8,128)(2,1)}, bf16[384,2048]{1,0:T(8,128)(2,1)}, u32[]{:S(2)}, u32[]{:S(2)}) collective-permute-start(bf16[384,2048]{1,0:T(8,128)(2,1)} %add_convert_fusion.4), channel_id=1, source_target_pairs={{0,2},{2,4},{5,3},{7,5},{8,10},{10,12},{13,11},{15,13},{16,18},{18... | collective-permute-start | bytes 4718600 | tf_op jit(solution)/shard_map/ppermute | solution.py:458
  74.4 9.9 %collective-permute-start.11 = (bf16[384,2048]{1,0:T(8,128)(2,1)S(1)}, bf16[384,2048]{1,0:T(8,128)(2,1)S(1)}, u32[]{:S(2)}, u32[]{:S(2)}) collective-permute-start(bf16[384,2048]{1,0:T(8,128)(2,1)S(1)} %collective-permute-done.10), channel_id=1, source_target_pairs={{0,1},{1,0},{2,3},{3,2},{4,5},{5,4},{6,7},{7,6},{8,9},{9,8},{10,11... | collective-permute-start | bytes 4718600 | tf_op jit(solution)/shard_map/ppermute | solution.py:453
  94.5 24.8 %collective-permute-start.12 = (bf16[384,2048]{1,0:T(8,128)(2,1)}, bf16[384,2048]{1,0:T(8,128)(2,1)}, u32[]{:S(2)}, u32[]{:S(2)}) collective-permute-start(bf16[384,2048]{1,0:T(8,128)(2,1)} %add_convert_fusion.3), channel_id=1, source_target_pairs={{0,2},{2,4},{4,6},{3,1},{5,3},{7,5},{8,10},{10,12},{12,14},{11,9},... | collective-permute-start | bytes 4718600 | tf_op jit(solution)/shard_map/ppermute | solution.py:458
  101.0 13.2 %copy-start.25 = (bf16[384,1024]{1,0:T(8,128)(2,1)S(1)}, bf16[384,1024]{1,0:T(8,128)(2,1)}, u32[]{:S(2)}) copy-start(bf16[384,1024]{1,0:T(8,128)(2,1)} %param.10) | copy-start | bytes 2359300
  114.5 2.4 collective-permute-start.13
  119.2 8.1 %copy-start.28 = (bf16[384,1024]{1,0:T(8,128)(2,1)S(1)}, bf16[384,1024]{1,0:T(8,128)(2,1)}, u32[]{:S(2)}) copy-start(bf16[384,1024]{1,0:T(8,128)(2,1)} %param.11) | copy-start | bytes 2359300
  121.7 5.7 %collective-permute-start.14 = (bf16[384,1024]{1,0:T(8,128)(2,1)}, bf16[384,1024]{1,0:T(8,128)(2,1)}, u32[]{:S(2)}, u32[]{:S(2)}) collective-permute-start(bf16[384,1024]{1,0:T(8,128)(2,1)} %fusion.7), channel_id=1, source_target_pairs={{0,1},{1,0},{2,3},{3,2},{4,5},{5,4},{6,7},{7,6},{8,9},{9,8},{10,11... | collective-permute-start | bytes 2359304 | tf_op jit(solution)/shard_map/ppermute | solution.py:453
  121.9 8.8 %copy-start.26 = (bf16[384,1024]{1,0:T(8,128)(2,1)S(1)}, bf16[384,1024]{1,0:T(8,128)(2,1)}, u32[]{:S(2)}) copy-start(bf16[384,1024]{1,0:T(8,128)(2,1)} %param.10) | copy-start | bytes 2359300
  121.9 27.1 %collective-permute-start.19 = (bf16[384,2048]{1,0:T(8,128)(2,1)}, bf16[384,2048]{1,0:T(8,128)(2,1)}, u32[]{:S(2)}, u32[]{:S(2)}) collective-permute-start(bf16[384,2048]{1,0:T(8,128)(2,1)} %get-tuple-element.95), channel_id=1, source_target_pairs={{0,2},{2,4},{4,6},{3,1},{5,3},{7,5},{8,10},{10,12},{12,14},{11,9},... | collective-permute-start | bytes 4718600 | tf_op jit(solution)/shard_map/ppermute | solution.py:458
  147.5 3.8 collective-permute-start.17
  147.5 37.6 %collective-permute-start.22 = (bf16[384,4096]{1,0:T(8,128)(2,1)}, bf16[384,4096]{1,0:T(8,128)(2,1)}, u32[]{:S(2)}, u32[]{:S(2)}) collective-permute-start(bf16[384,4096]{1,0:T(8,128)(2,1)} %column_half.2), channel_id=1, source_target_pairs={{0,8},{1,17},{2,10},{3,19},{4,12},{5,21},{6,14},{7,23},{8,0},{9,25... | collective-permute-start | bytes 9437192 | tf_op jit(solution)/shard_map/ppermute | solution.py:562
  149.0 39.4 %collective-permute-start.20 = (bf16[384,2048]{1,0:T(8,128)(2,1)}, bf16[384,2048]{1,0:T(8,128)(2,1)S(1)}, u32[]{:S(2)}, u32[]{:S(2)}) collective-permute-start(bf16[384,2048]{1,0:T(8,128)(2,1)} %collective-permute-done.19), channel_id=1, source_target_pairs={{2,4},{4,6},{3,1},{5,3},{10,12},{12,14},{11,9},{13,11},{18,20},{20... | collective-permute-start | bytes 4718600 | tf_op jit(solution)/shard_map/ppermute | solution.py:458
  149.8 52.1 %collective-permute-start.24 = (bf16[384,2048]{1,0:T(8,128)(2,1)}, bf16[384,2048]{1,0:T(8,128)(2,1)S(1)}, u32[]{:S(2)}, u32[]{:S(2)}) collective-permute-start(bf16[384,2048]{1,0:T(8,128)(2,1)} %collective-permute-done.19), channel_id=1, source_target_pairs={{0,1},{1,0},{2,3},{3,2},{4,5},{5,4},{6,7},{7,6},{8,9},{9,8},{10,11... | collective-permute-start | bytes 4718600 | tf_op jit(solution)/shard_map/ppermute | solution.py:453
  150.6 53.6 %collective-permute-start.16 = (bf16[96,8192]{1,0:T(8,128)(2,1)}, bf16[96,8192]{1,0:T(8,128)(2,1)S(1)}, u32[]{:S(2)}, u32[]{:S(2)}) collective-permute-start(bf16[96,8192]{1,0:T(8,128)(2,1)} %get-tuple-element.103), channel_id=1, source_target_pairs={{0,1},{1,0},{2,3},{3,2},{4,5},{5,4},{6,7},{7,6},{8,9},{9,8},{10,11... | collective-permute-start | bytes 4718600 | tf_op jit(solution)/shard_map/ppermute | solution.py:453
  151.3 35.3 %copy-start.21 = (bf16[384,2048]{1,0:T(8,128)(2,1)S(1)}, bf16[384,2048]{1,0:T(8,128)(2,1)}, u32[]{:S(2)}) copy-start(bf16[384,2048]{1,0:T(8,128)(2,1)} %get-tuple-element.95) | copy-start | bytes 4718596
  155.8 48.0 %collective-permute-start.18 = (bf16[96,8192]{1,0:T(8,128)(2,1)S(1)}, bf16[96,8192]{1,0:T(8,128)(2,1)S(1)}, u32[]{:S(2)}, u32[]{:S(2)}) collective-permute-start(bf16[96,8192]{1,0:T(8,128)(2,1)S(1)} %get-tuple-element.96), channel_id=1, source_target_pairs={{0,2},{7,5},{8,10},{15,13},{16,18},{23,21},{24,26},{31,29}} | collective-permute-start | bytes 4718600 | tf_op jit(solution)/shard_map/ppermute | solution.py:458
  162.4 26.0 %copy-start.17 = (bf16[2,256,384]{2,1,0:T(8,128)(2,1)}, bf16[2,256,384]{2,1,0:T(8,128)(2,1)S(1)}, u32[]{:S(2)}) copy-start(bf16[2,256,384]{2,1,0:T(8,128)(2,1)S(1)} %get-tuple-element.81) | copy-start | bytes 1179652
  162.4 31.3 %copy-start.15 = (bf16[1024,384]{1,0:T(8,128)(2,1)}, bf16[1024,384]{1,0:T(8,128)(2,1)S(1)}, u32[]{:S(2)}) copy-start(bf16[1024,384]{1,0:T(8,128)(2,1)S(1)} %get-tuple-element.63.refs_0_.refs_1_) | copy-start | bytes 2359300
  185.1 7.8 %collective-permute-start.21 = (bf16[2,256,384]{2,1,0:T(8,128)(2,1)S(1)}, bf16[2,256,384]{2,1,0:T(8,128)(2,1)S(1)}, u32[]{:S(2)}, u32[]{:S(2)}) collective-permute-start(bf16[2,256,384]{2,1,0:T(8,128)(2,1)S(1)} %get-tuple-element.66), channel_id=1, source_target_pairs={{0,8},{1,17},{2,10},{3,19},{4,12},{5,21},{6,14},{7,23},{8,0},{9,25... | collective-permute-start | bytes 1179656 | tf_op jit(solution)/shard_map/ppermute | solution.py:562
  188.4 87.4 %collective-permute-start.36 = (bf16[384,4096]{1,0:T(8,128)(2,1)}, bf16[384,4096]{1,0:T(8,128)(2,1)}, u32[]{:S(2)}, u32[]{:S(2)}) collective-permute-start(bf16[384,4096]{1,0:T(8,128)(2,1)} %collective-permute-done.22.refs_4_), channel_id=1, source_target_pairs={{0,1},{1,0},{2,3},{3,2},{4,5},{5,4},{6,7},{7,6},{8,9},{9,8},{10,11... | collective-permute-start | bytes 9437192 | tf_op jit(solution)/shard_map/ppermute | solution.py:453
  192.9 14.5 %collective-permute-start.26 = (bf16[384,2048]{1,0:T(8,128)(2,1)S(1)}, bf16[384,2048]{1,0:T(8,128)(2,1)S(1)}, u32[]{:S(2)}, u32[]{:S(2)}) collective-permute-start(bf16[384,2048]{1,0:T(8,128)(2,1)S(1)} %collective-permute-done.20), channel_id=1, source_target_pairs={{4,6},{3,1},{12,14},{11,9},{20,22},{19,17},{28,30},{27,25}} | collective-permute-start | bytes 4718600 | tf_op jit(solution)/shard_map/ppermute | solution.py:458
  201.9 15.7 %collective-permute-start.25 = (bf16[384,2048]{1,0:T(8,128)(2,1)S(1)}, bf16[384,2048]{1,0:T(8,128)(2,1)S(1)}, u32[]{:S(2)}, u32[]{:S(2)}) collective-permute-start(bf16[384,2048]{1,0:T(8,128)(2,1)S(1)} %collective-permute-done.20), channel_id=1, source_target_pairs={{0,1},{1,0},{2,3},{3,2},{4,5},{5,4},{6,7},{7,6},{8,9},{9,8},{10,11... | collective-permute-start | bytes 4718600 | tf_op jit(solution)/shard_map/ppermute | solution.py:453
  203.8 30.9 %collective-permute-start.15 = (bf16[96,8192]{1,0:T(8,128)(2,1)}, bf16[96,8192]{1,0:T(8,128)(2,1)}, u32[]{:S(2)}, u32[]{:S(2)}) collective-permute-start(bf16[96,8192]{1,0:T(8,128)(2,1)} %get-tuple-element.97), channel_id=1, source_target_pairs={{0,1},{1,0},{2,3},{3,2},{4,5},{5,4},{6,7},{7,6},{8,9},{9,8},{10,11... | collective-permute-start | bytes 4718600 | tf_op jit(solution)/shard_map/ppermute | solution.py:453
  207.4 13.7 %collective-permute-start.27 = (bf16[384,2048]{1,0:T(8,128)(2,1)S(1)}, bf16[384,2048]{1,0:T(8,128)(2,1)S(1)}, u32[]{:S(2)}, u32[]{:S(2)}) collective-permute-start(bf16[384,2048]{1,0:T(8,128)(2,1)S(1)} %collective-permute-done.26), channel_id=1, source_target_pairs={{0,1},{1,0},{2,3},{3,2},{4,5},{5,4},{6,7},{7,6},{8,9},{9,8},{10,11... | collective-permute-start | bytes 4718600 | tf_op jit(solution)/shard_map/ppermute | solution.py:453
  214.7 20.0 %collective-permute-start.23 = (bf16[96,8192]{1,0:T(8,128)(2,1)}, bf16[96,8192]{1,0:T(8,128)(2,1)}, u32[]{:S(2)}, u32[]{:S(2)}) collective-permute-start(bf16[96,8192]{1,0:T(8,128)(2,1)} %add_convert_fusion.1), channel_id=1, source_target_pairs={{0,2},{2,4},{5,3},{7,5},{8,10},{10,12},{13,11},{15,13},{16,18},{18... | collective-permute-start | bytes 4718600 | tf_op jit(solution)/shard_map/ppermute | solution.py:458
  227.1 37.6 %collective-permute-start.31 = (bf16[384,4096]{1,0:T(8,128)(2,1)}, bf16[384,4096]{1,0:T(8,128)(2,1)}, u32[]{:S(2)}, u32[]{:S(2)}) collective-permute-start(bf16[384,4096]{1,0:T(8,128)(2,1)} %column_half.3), channel_id=1, source_target_pairs={{0,8},{1,17},{2,10},{3,19},{4,12},{5,21},{6,14},{7,23},{8,0},{9,25... | collective-permute-start | bytes 9437192 | tf_op jit(solution)/shard_map/ppermute | solution.py:562
  238.8 24.7 %collective-permute-start.28 = (bf16[96,8192]{1,0:T(8,128)(2,1)}, bf16[96,8192]{1,0:T(8,128)(2,1)}, u32[]{:S(2)}, u32[]{:S(2)}) collective-permute-start(bf16[96,8192]{1,0:T(8,128)(2,1)} %add_convert_fusion), channel_id=1, source_target_pairs={{0,2},{2,4},{4,6},{3,1},{5,3},{7,5},{8,10},{10,12},{12,14},{11,9},... | collective-permute-start | bytes 4718600 | tf_op jit(solution)/shard_map/ppermute | solution.py:458
  246.4 13.3 %copy-start.23 = (f32[384,1024]{1,0:T(8,128)S(1)}, f32[384,1024]{1,0:T(8,128)}, u32[]{:S(2)}) copy-start(f32[384,1024]{1,0:T(8,128)} %copy-done.22) | copy-start | bytes 4718596
  246.5 13.3 %copy-start.29 = (bf16[384,1024]{1,0:T(8,128)(2,1)S(1)}, bf16[384,1024]{1,0:T(8,128)(2,1)}, u32[]{:S(2)}) copy-start(bf16[384,1024]{1,0:T(8,128)(2,1)} %param.11) | copy-start | bytes 2359300
  261.3 6.9 %copy-start.37 = (s32[128]{0:T(128)S(1)}, s32[128]{0:T(128)}, u32[]{:S(2)}) copy-start(s32[128]{0:T(128)} %param.15) | copy-start | bytes 1540
  261.3 16.1 %copy-start.16 = (bf16[1024,384]{1,0:T(8,128)(2,1)S(1)}, bf16[1024,384]{1,0:T(8,128)(2,1)}, u32[]{:S(2)}) copy-start(bf16[1024,384]{1,0:T(8,128)(2,1)} %copy-done.15) | copy-start | bytes 2359300
  264.7 63.0 %collective-permute-start.33 = (bf16[384,4096]{1,0:T(8,128)(2,1)}, bf16[384,4096]{1,0:T(8,128)(2,1)}, u32[]{:S(2)}, u32[]{:S(2)}) collective-permute-start(bf16[384,4096]{1,0:T(8,128)(2,1)} %collective-permute-done.31.refs_4_), channel_id=1, source_target_pairs={{0,1},{1,0},{2,3},{3,2},{4,5},{5,4},{6,7},{7,6},{8,9},{9,8},{10,11... | collective-permute-start | bytes 9437192 | tf_op jit(solution)/shard_map/ppermute | solution.py:453
  266.0 26.9 %collective-permute-start.29 = (bf16[48,8192]{1,0:T(8,128)(2,1)S(1)}, bf16[48,8192]{1,0:T(8,128)(2,1)S(1)}, u32[]{:S(2)}, u32[]{:S(2)}) collective-permute-start(bf16[48,8192]{1,0:T(8,128)(2,1)S(1)} %fusion.5), channel_id=1, source_target_pairs={{0,1},{1,0},{2,3},{3,2},{4,5},{5,4},{6,7},{7,6},{8,9},{9,8},{10,11... | collective-permute-start | bytes 2359304 | tf_op jit(solution)/shard_map/ppermute | solution.py:453
  266.6 7.8 %collective-permute-start.35 = (bf16[2,256,384]{2,1,0:T(8,128)(2,1)S(1)}, bf16[2,256,384]{2,1,0:T(8,128)(2,1)S(1)}, u32[]{:S(2)}, u32[]{:S(2)}) collective-permute-start(bf16[2,256,384]{2,1,0:T(8,128)(2,1)S(1)} %copy-done.18), channel_id=1, source_target_pairs={{0,16},{1,9},{2,18},{3,11},{4,20},{5,13},{6,22},{7,15},{8,24},{9,1... | collective-permute-start | bytes 1179656 | tf_op jit(solution)/shard_map/ppermute | solution.py:562
  269.2 58.5 %collective-permute-start.32 = (bf16[2,256,384]{2,1,0:T(8,128)(2,1)S(1)}, bf16[2,256,384]{2,1,0:T(8,128)(2,1)}, u32[]{:S(2)}, u32[]{:S(2)}) collective-permute-start(bf16[2,256,384]{2,1,0:T(8,128)(2,1)S(1)} %get-tuple-element.76), channel_id=1, source_target_pairs={{0,16},{1,9},{2,18},{3,11},{4,20},{5,13},{6,22},{7,15},{8,24},{9,1... | collective-permute-start | bytes 1179656 | tf_op jit(solution)/shard_map/ppermute | solution.py:562
  274.4 43.1 %collective-permute-start.30 = (bf16[2,256,384]{2,1,0:T(8,128)(2,1)}, bf16[2,256,384]{2,1,0:T(8,128)(2,1)}, u32[]{:S(2)}, u32[]{:S(2)}) collective-permute-start(bf16[2,256,384]{2,1,0:T(8,128)(2,1)} %get-tuple-element.73), channel_id=1, source_target_pairs={{0,8},{1,17},{2,10},{3,19},{4,12},{5,21},{6,14},{7,23},{8,0},{9,25... | collective-permute-start | bytes 1179656 | tf_op jit(solution)/shard_map/ppermute | solution.py:562
  275.9 66.7 %collective-permute-start.34 = (bf16[256,4096]{1,0:T(8,128)(2,1)}, bf16[256,4096]{1,0:T(8,128)(2,1)}, u32[]{:S(2)}, u32[]{:S(2)}) collective-permute-start(bf16[256,4096]{1,0:T(8,128)(2,1)} %get-tuple-element.79), channel_id=1, source_target_pairs={{0,16},{1,9},{2,18},{3,11},{4,20},{5,13},{6,22},{7,15},{8,24},{9,1... | collective-permute-start | bytes 6291464 | tf_op jit(solution)/shard_map/ppermute | solution.py:562
  287.0 26.9 %all-to-all-start = ((bf16[8,48,1024]{2,1,0:T(8,128)(2,1)}), bf16[8,48,1024]{2,1,0:T(8,128)(2,1)S(1)}, u32[]{:S(2)}, u32[]{:S(2)}) async-start(bf16[8,48,1024]{2,1,0:T(8,128)(2,1)} %bitcast.16), calls=%async_computation | async-start | bytes 1572864 | tf_op jit(solution)/shard_map/all_to_all | solution.py:672
  293.0 49.7 %collective-permute-start.37 = (bf16[256,4096]{1,0:T(8,128)(2,1)}, bf16[256,4096]{1,0:T(8,128)(2,1)}, u32[]{:S(2)}, u32[]{:S(2)}) collective-permute-start(bf16[256,4096]{1,0:T(8,128)(2,1)} %get-tuple-element.83), channel_id=1, source_target_pairs={{0,8},{1,17},{2,10},{3,19},{4,12},{5,21},{6,14},{7,23},{8,0},{9,25... | collective-permute-start | bytes 6291464 | tf_op jit(solution)/shard_map/ppermute | solution.py:562
  295.2 22.3 %copy-start.14 = (bf16[1024,384]{1,0:T(8,128)(2,1)S(1)}, bf16[1024,384]{1,0:T(8,128)(2,1)}, u32[]{:S(2)}) copy-start(bf16[1024,384]{1,0:T(8,128)(2,1)} %copy-done.13) | copy-start | bytes 2359300
  327.2 92.6 %collective-permute-start.38 = (bf16[256,4096]{1,0:T(8,128)(2,1)}, bf16[256,4096]{1,0:T(8,128)(2,1)}, u32[]{:S(2)}, u32[]{:S(2)}) collective-permute-start(bf16[256,4096]{1,0:T(8,128)(2,1)} %get-tuple-element.88), channel_id=1, source_target_pairs={{0,16},{1,9},{2,18},{3,11},{4,20},{5,13},{6,22},{7,15},{8,24},{9,1... | collective-permute-start | bytes 6291464 | tf_op jit(solution)/shard_map/ppermute | solution.py:562
  327.7 13.9 %copy-start.36 = (f32[2,256]{1,0:T(2,128)S(1)}, f32[2,256]{1,0:T(2,128)}, u32[]{:S(2)}) copy-start(f32[2,256]{1,0:T(2,128)} %param.14) | copy-start | bytes 6148
  327.7 14.0 %copy-start.33 = (s32[4,1536,4]{1,2,0:T(4,128)S(1)}, s32[4,1536,4]{1,2,0:T(4,128)}, u32[]{:S(2)}) copy-start(s32[4,1536,4]{1,2,0:T(4,128)} %param.16) | copy-start | bytes 294916
  327.7 14.0 %copy-start.34 = (s32[4,1536]{1,0:T(4,128)S(1)}, s32[4,1536]{1,0:T(4,128)}, u32[]{:S(2)}) copy-start(s32[4,1536]{1,0:T(4,128)} %param.17) | copy-start | bytes 73732
  337.5 82.3 %collective-permute-start.39 = (bf16[256,4096]{1,0:T(8,128)(2,1)}, bf16[256,4096]{1,0:T(8,128)(2,1)}, u32[]{:S(2)}, u32[]{:S(2)}) collective-permute-start(bf16[256,4096]{1,0:T(8,128)(2,1)} %get-tuple-element.89), channel_id=1, source_target_pairs={{0,8},{1,17},{2,10},{3,19},{4,12},{5,21},{6,14},{7,23},{8,0},{9,25... | collective-permute-start | bytes 6291464 | tf_op jit(solution)/shard_map/ppermute | solution.py:562
  338.0 46.1 %all-to-all-start.1 = ((bf16[32,2,48,128]{3,2,1,0:T(8,128)(2,1)}), bf16[32,2,48,128]{3,2,1,0:T(8,128)(2,1)S(1)}, u32[]{:S(2)}, u32[]{:S(2)}) async-start(bf16[32,2,48,128]{3,2,1,0:T(8,128)(2,1)} %to_slots.1), calls=%async_computation.1 | async-start | bytes 1572864 | tf_op jit(solution)/shard_map/all_to_all | solution.py:687
  385.0 34.8 %copy-start.10 = (bf16[256,4096]{1,0:T(8,128)(2,1)S(1)}, bf16[256,4096]{1,0:T(8,128)(2,1)}, u32[]{:S(2)}) copy-start(bf16[256,4096]{1,0:T(8,128)(2,1)} %copy-done.9) | copy-start | bytes 6291460
  385.0 34.8 %copy-start.12 = (bf16[256,4096]{1,0:T(8,128)(2,1)S(1)}, bf16[256,4096]{1,0:T(8,128)(2,1)}, u32[]{:S(2)}) copy-start(bf16[256,4096]{1,0:T(8,128)(2,1)} %copy-done.11) | copy-start | bytes 6291460
  (16 other events, 42.0 us)
